TPU v7x, 256 devices: a whole 4x4x8 slice. The times are simulated.
256 devices in a mesh: sec: 2 (over z_lo), lat: 8 (over y, core), lon: 16 (over z_hi, x).
Axes of the slice: x: 4, y: 4, z: 8 (z_hi: 4, z_lo: 2; z = z_hi * 2 + z_lo), core: 2. Of those that a mesh axis runs over, the one named last changes fastest.
Arguments:
- ocean_state: bfloat16 [4, 2, 8, 32, 128], P(None, 'sec', 'lat', 'lon'), may hold values from -4 to 4
- sea_tiles: int32 [2, 8, 32], P('sec', 'lat', 'lon'), may hold values 0 or 1
- regrid_weights: bfloat16 [64, 4, 128, 4096], P('lat', None, None, 'lon'), may hold values from -0.25 to 0.25
- regrid_src: int32 [64, 16, 4], P('lat', 'lon'), may hold values from 0 to 11
- row_points: int32 [64], P('lat'), may hold values from 1040 to 4096, as said below
- wind: float32 [2, 64, 4096], P(None, 'lat', 'lon'), may hold values from -3 to 3
- conc: bfloat16 [32, 20, 64, 4096], P(None, 'sec', 'lat', 'lon'), may hold values from 0.049804688 to 2
- kdiff: float32 [32, 64, 4096], P(None, 'lat', 'lon'), may hold values from 0.1 to 10
- bin_emit: float32 [20], P('sec'), may hold values from 0.05 to 0.5
- bin_settle: float32 [20], P('sec'), may hold values from 0.1 to 2
- bin_mass: float32 [20], P('sec'), may hold values from 0.2 to 2
Outputs:
- spectra: float32 [32, 20, 64, 2, 1280], P('lon', 'sec', 'lat')
- salt_flux: float32 [64, 4096], P('lat', 'lon')
Inputs may be any that keep to these rules, and one draw needn't show every extreme that they name: `regrid_src`: slot k names ocean section k // 6, tile offset (k // 2) % 3 - 1 and block k % 2. `row_points`: a multiple of 16.
All inputs are finite; a program needn't handle non-finite values. No bound on the sum of `sea_tiles` on one device may be relied on, other than what follows from the above.
Results may differ from a plain program's by a relative error of at most 0.0019.
Values may be sent and summed in bfloat16 or wider, within the bound.
A program may use at most 128 MiB of HBM per device.

v0:
```python
import math

import jax
import jax.numpy as jnp
import numpy as np
from jax import lax
from jax.sharding import PartitionSpec as P

M = 4096
K = 1280
LEV = 32


def padded(block, sides, width):
    for axis, dim in sides:
        count = lax.axis_size(axis)
        forward = [(i, i + 1) for i in range(count - 1)]
        forward.append((count - 1, 0))
        backward = [(target, source) for source, target in forward]
        low = lax.ppermute(
            lax.slice_in_dim(block, block.shape[dim] - width, None, axis=dim), axis, forward
        )
        high = lax.ppermute(lax.slice_in_dim(block, 0, width, axis=dim), axis, backward)
        block = jnp.concatenate([low, block, high], axis=dim)
    return block


def from_partner(value, axis, apart):
    mask = 2**apart
    pairs = [(source, source ^ mask) for source in range(lax.axis_size(axis))]
    return lax.ppermute(value, axis, pairs)


def solve_columns(concentration, kdiff, bin_flux, settle_rate):
    levels_count = concentration.shape[0]
    ratios = []
    scaled = []
    ratio_prev = 0.0
    scaled_prev = 0.0
    for level in range(levels_count):
        level_conc = concentration[level].astype(jnp.float32)
        here_kdiff = kdiff[level]
        if level == levels_count - 1:
            diagonal = 1.0 + here_kdiff + settle_rate
            right_side = level_conc + bin_flux
        else:
            diagonal = 1.0 + here_kdiff + kdiff[level + 1]
            right_side = level_conc
        pivots = diagonal - here_kdiff * ratio_prev
        if level == levels_count - 1:
            ratio_now = 0.0
        else:
            ratio_now = kdiff[level + 1] / pivots
        scaled_now = (right_side + here_kdiff * scaled_prev) / pivots
        ratios.append(ratio_now)
        scaled.append(scaled_now)
        ratio_prev = ratio_now
        scaled_prev = scaled_now
    values = [None] * levels_count
    carried = 0.0
    for level in range(levels_count - 1, -1, -1):
        carried = scaled[level] + ratios[level] * carried
        values[level] = carried
    return jnp.stack(values, axis=0)


def emission_base(fields, wind, valid):
    rel_east = wind[0] - 0.5 * fields[2]
    rel_north = wind[1] - 0.5 * fields[3]
    wind_speed = jnp.sqrt(rel_east * rel_east + rel_north * rel_north + 0.25)
    open_water = 1.0 - jax.nn.sigmoid(fields[1])
    return (
        open_water * jnp.exp(3.41 * jnp.log(wind_speed)) * (0.5 + jax.nn.sigmoid(fields[0])) * valid
    )


def order_pair(own_part, partner, sec_index, axis_pos):
    first_half = jnp.where(sec_index == 0, own_part, partner)
    second_half = jnp.where(sec_index == 0, partner, own_part)
    return jnp.stack([first_half, second_half], axis=axis_pos)


def neighbour_tiles(ocean_state, sea_tiles):
    field_count = ocean_state.shape[0]
    blocks_dev = ocean_state.shape[3]
    block_width = ocean_state.shape[4]
    masked = ocean_state.reshape(field_count, blocks_dev, block_width) * sea_tiles.reshape(
        1, blocks_dev, 1
    ).astype(jnp.bfloat16)
    sec_index = lax.axis_index("sec")
    widened = padded(masked, (("lon", 1),), blocks_dev)
    partner = from_partner(widened, "sec", 0)
    paired = order_pair(widened, partner, sec_index, 1)
    return paired.reshape(field_count, 6 * blocks_dev, block_width)


def whole_tables():
    product = np.arange(M)[:, None] * np.arange(K)[None, :] % M
    angles = product * (2.0 * np.pi / M)
    trig_table = np.stack([np.cos(angles), -np.sin(angles)], axis=1).astype(np.float32)
    table_full = jnp.asarray(trig_table)
    table_high = table_full.astype(jnp.bfloat16)
    table_low = (table_full - table_high.astype(jnp.float32)).astype(jnp.bfloat16)
    return (table_high, table_low)


def transform(block_rows, table_high, table_low):
    high_part = jnp.einsum(
        "lbrm,mck->lbrck", block_rows, table_high, preferred_element_type=jnp.float32
    )
    low_part = jnp.einsum(
        "lbrm,mck->lbrck", block_rows, table_low, preferred_element_type=jnp.float32
    )
    return (high_part + low_part) * (1.0 / math.sqrt(M))


def on_device(
    ocean_state,
    sea_tiles,
    regrid_weights,
    regrid_src,
    row_points,
    wind,
    conc,
    kdiff,
    bin_emit,
    bin_settle,
    bin_mass,
):
    ocean_tiles = neighbour_tiles(ocean_state, sea_tiles)
    rows_dev = wind.shape[1]
    points_dev = wind.shape[2]
    sources = regrid_src.reshape(rows_dev, regrid_src.shape[2])
    slot_ids = jnp.arange(ocean_tiles.shape[1], dtype=jnp.int32)
    selector = (sources[:, :, None] == slot_ids[None, None, :]).astype(jnp.bfloat16)
    chosen = jnp.einsum(
        "rsk,fkq->frsq", selector, ocean_tiles, preferred_element_type=jnp.float32
    ).astype(jnp.bfloat16)
    fields = jnp.einsum(
        "frsq,rsqp->frp", chosen, regrid_weights, preferred_element_type=jnp.float32
    )
    columns = lax.axis_index("lon") * points_dev + jnp.arange(points_dev, dtype=jnp.int32)
    valid = (columns[None, :] < row_points[:, None]).astype(jnp.float32)
    base_rate = emission_base(fields, wind, valid)
    bin_flux = bin_emit[:, None, None] * base_rate[None]
    settle_rate = bin_settle[:, None, None]
    mixed = solve_columns(conc, kdiff[:, None], bin_flux, settle_rate)
    net_flux = bin_flux - settle_rate * mixed[LEV - 1]
    partial_salt = jnp.sum(bin_mass[:, None, None] * net_flux, axis=0)
    salt_flux = lax.psum(partial_salt, "sec") * valid
    spectral_in = mixed.astype(jnp.bfloat16) * valid.astype(jnp.bfloat16)
    whole_high, whole_low = whole_tables()
    spectra = transform(
        lax.all_to_all(spectral_in, "lon", split_axis=0, concat_axis=3, tiled=True),
        whole_high,
        whole_low,
    )
    return (spectra, salt_flux)


def solution(mesh):
    return jax.shard_map(
        on_device,
        mesh=mesh,
        in_specs=(
            P(None, "sec", "lat", "lon", None),
            P("sec", "lat", "lon"),
            P("lat", None, None, "lon"),
            P("lat", "lon", None),
            P("lat"),
            P(None, "lat", "lon"),
            P(None, "sec", "lat", "lon"),
            P(None, "lat", "lon"),
            P("sec"),
            P("sec"),
            P("sec"),
        ),
        out_specs=(P("lon", "sec", "lat", None, None), P("lat", "lon")),
        check_vma=False,
    )
```

profile of v0, /device:TPU:16, one launch (start us, length us, event | category | flops | bytes accessed | tf_op | source)
XLA Modules:
  0.0 109.1 jit_solution(5937875934413156654)
XLA Ops:
  0.7 0.8 convert_bitcast_fusion.32
  1.5 0.8 bitcast_multiply_fusion
  2.2 8.5 %collective-permute-start.1 = (bf16[4,2,128]{2,1,0:T(2,128)(2,1)S(1)}, bf16[4,2,128]{2,1,0:T(2,128)(2,1)S(1)}, u32[]{:S(2)}, u32[]{:S(2)}) collective-permute-start(bf16[4,2,128]{2,1,0:T(2,128)(2,1)S(1)} %bitcast_multiply_fusion), channel_id=1, source_target_pairs={{1,0},{2,1},{3,2},{4,3},{5,4},{6,5},{7,6},{8,7},{9,8},{10,9},{11,1... | collective-permute-start | bytes 6152 | tf_op jit(solution)/shard_map/ppermute | solution.py:23
  10.7 1.4 %fusion.147 = (f32[8,256]{1,0:T(8,128)}, f32[1,8,256]{2,1,0:T(8,128)S(1)}, f32[1,8,256]{2,1,0:T(8,128)S(1)}) fusion(f32[32,8,256]{2,1,0:T(8,128)} %param.19), kind=kLoop, calls=%fused_computation.390 | loop fusion | flops 30720 | bytes 57344 | tf_op jit(solution)/shard_map/mul | solution.py:62
  12.1 1.4 %fusion.149 = (f32[8,256]{1,0:T(8,128)}, f32[1,8,256]{2,1,0:T(8,128)S(1)}, f32[1,8,256]{2,1,0:T(8,128)S(1)}) fusion(f32[32,8,256]{2,1,0:T(8,128)} %param.19, f32[1,8,256]{2,1,0:T(8,128)S(1)} %get-tuple-element.39), kind=kLoop, calls=%fused_computation.392 | loop fusion | flops 22528 | bytes 57344 | tf_op jit(solution)/shard_map/mul | solution.py:62
  13.5 1.4 %fusion.151 = (f32[8,256]{1,0:T(8,128)}, f32[1,8,256]{2,1,0:T(8,128)S(1)}, f32[1,8,256]{2,1,0:T(8,128)S(1)}) fusion(f32[32,8,256]{2,1,0:T(8,128)} %param.19, f32[1,8,256]{2,1,0:T(8,128)S(1)} %get-tuple-element.42), kind=kLoop, calls=%fused_computation.394 | loop fusion | flops 22528 | bytes 57344 | tf_op jit(solution)/shard_map/mul | solution.py:62
  14.8 1.3 %fusion.153 = (f32[8,256]{1,0:T(8,128)}, f32[1,8,256]{2,1,0:T(8,128)S(1)}, f32[1,8,256]{2,1,0:T(8,128)S(1)}) fusion(f32[32,8,256]{2,1,0:T(8,128)} %param.19, f32[1,8,256]{2,1,0:T(8,128)S(1)} %get-tuple-element.45), kind=kLoop, calls=%fused_computation.396 | loop fusion | flops 22528 | bytes 57344 | tf_op jit(solution)/shard_map/mul | solution.py:62
  16.2 1.3 %fusion.155 = (f32[8,256]{1,0:T(8,128)}, f32[1,8,256]{2,1,0:T(8,128)S(1)}, f32[1,8,256]{2,1,0:T(8,128)S(1)}) fusion(f32[32,8,256]{2,1,0:T(8,128)} %param.19, f32[1,8,256]{2,1,0:T(8,128)S(1)} %get-tuple-element.48), kind=kLoop, calls=%fused_computation.398 | loop fusion | flops 22528 | bytes 57344 | tf_op jit(solution)/shard_map/mul | solution.py:62
  17.5 1.4 %fusion.157 = (f32[8,256]{1,0:T(8,128)}, f32[1,8,256]{2,1,0:T(8,128)S(1)}, f32[1,8,256]{2,1,0:T(8,128)S(1)}) fusion(f32[32,8,256]{2,1,0:T(8,128)} %param.19, f32[1,8,256]{2,1,0:T(8,128)S(1)} %get-tuple-element.51), kind=kLoop, calls=%fused_computation.400 | loop fusion | flops 22528 | bytes 57344 | tf_op jit(solution)/shard_map/mul | solution.py:62
  18.9 1.6 %fusion.159 = (f32[8,256]{1,0:T(8,128)}, f32[1,8,256]{2,1,0:T(8,128)S(1)}, f32[1,8,256]{2,1,0:T(8,128)S(1)}, f32[8,256]{1,0:T(8,128)}, f32[8,256]{1,0:T(8,128)},...) fusion(f32[32,8,256]{2,1,0:T(8,128)} %param.19, ...), kind=kLoop, calls=%fused_computation.402 | loop fusion | flops 22528 | bytes 294912 | tf_op jit(solution)/shard_map/mul | solution.py:62
  20.5 1.4 %fusion.161 = (f32[8,256]{1,0:T(8,128)}, f32[1,8,256]{2,1,0:T(8,128)S(1)}, f32[1,8,256]{2,1,0:T(8,128)S(1)}, f32[8,256]{1,0:T(8,128)S(1)}, f32[8,256]{1,0:T(8,128)S(1)}, /*index=5*/f32[8,256]{1,0:T(8,128)S(1)}) fusion(f32[32,8,256]{2,1,0:T(8,128)} %param.19, f32[1,8,256]{2,1,0:T(8,128)S(1)} %get-tuple-element.57), kind=kLoop, calls=%fused_computation.404 | loop fusion | flops 24576 | bytes 98304 | tf_op jit(solution)/shard_map/mul | solution.py:62
  21.9 1.4 %fusion.163 = (f32[8,256]{1,0:T(8,128)}, f32[1,8,256]{2,1,0:T(8,128)S(1)}, f32[1,8,256]{2,1,0:T(8,128)S(1)}) fusion(f32[32,8,256]{2,1,0:T(8,128)} %param.19, f32[1,8,256]{2,1,0:T(8,128)S(1)} %get-tuple-element.60), kind=kLoop, calls=%fused_computation.406 | loop fusion | flops 22528 | bytes 57344 | tf_op jit(solution)/shard_map/mul | solution.py:62
  23.2 1.4 %fusion.165 = (f32[8,256]{1,0:T(8,128)}, f32[1,8,256]{2,1,0:T(8,128)S(1)}, f32[1,8,256]{2,1,0:T(8,128)S(1)}) fusion(f32[32,8,256]{2,1,0:T(8,128)} %param.19, f32[1,8,256]{2,1,0:T(8,128)S(1)} %get-tuple-element.63), kind=kLoop, calls=%fused_computation.408 | loop fusion | flops 22528 | bytes 57344 | tf_op jit(solution)/shard_map/mul | solution.py:62
  24.6 1.4 %fusion.167 = (f32[8,256]{1,0:T(8,128)}, f32[1,8,256]{2,1,0:T(8,128)S(1)}, f32[1,8,256]{2,1,0:T(8,128)S(1)}) fusion(f32[32,8,256]{2,1,0:T(8,128)} %param.19, f32[1,8,256]{2,1,0:T(8,128)S(1)} %get-tuple-element.66), kind=kLoop, calls=%fused_computation.410 | loop fusion | flops 22528 | bytes 57344 | tf_op jit(solution)/shard_map/mul | solution.py:62
  26.0 1.4 %fusion.169 = (f32[8,256]{1,0:T(8,128)}, f32[1,8,256]{2,1,0:T(8,128)S(1)}, f32[1,8,256]{2,1,0:T(8,128)S(1)}) fusion(f32[32,8,256]{2,1,0:T(8,128)} %param.19, f32[1,8,256]{2,1,0:T(8,128)S(1)} %get-tuple-element.69), kind=kLoop, calls=%fused_computation.412 | loop fusion | flops 22528 | bytes 57344 | tf_op jit(solution)/shard_map/mul | solution.py:62
  27.3 1.4 %fusion.171 = (f32[8,256]{1,0:T(8,128)}, f32[1,8,256]{2,1,0:T(8,128)S(1)}, f32[1,8,256]{2,1,0:T(8,128)S(1)}) fusion(f32[32,8,256]{2,1,0:T(8,128)} %param.19, f32[1,8,256]{2,1,0:T(8,128)S(1)} %get-tuple-element.72), kind=kLoop, calls=%fused_computation.414 | loop fusion | flops 22528 | bytes 57344 | tf_op jit(solution)/shard_map/mul | solution.py:62
  28.7 1.4 %fusion.173 = (f32[8,256]{1,0:T(8,128)}, f32[1,8,256]{2,1,0:T(8,128)S(1)}, f32[1,8,256]{2,1,0:T(8,128)S(1)}) fusion(f32[32,8,256]{2,1,0:T(8,128)} %param.19, f32[1,8,256]{2,1,0:T(8,128)S(1)} %get-tuple-element.75), kind=kLoop, calls=%fused_computation.416 | loop fusion | flops 22528 | bytes 57344 | tf_op jit(solution)/shard_map/mul | solution.py:62
  30.1 1.5 %multiply_bitcast_fusion = (f32[8,256]{1,0:T(8,128)S(1)}, f32[1,8,256]{2,1,0:T(8,128)S(1)}, f32[1,8,256]{2,1,0:T(8,128)S(1)}, f32[8,256]{1,0:T(8,128)}, f32[8,25...) fusion(f32[32,8,256]{2,1,0:T(8,128)} %param.19, ...), kind=kLoop, calls=%fused_computation.285 | loop fusion | flops 40960 | bytes 221184 | tf_op jit(solution)/shard_map/sub | solution.py:49
  31.6 0.7 fusion.174
  32.2 0.7 fusion.145
  33.0 1.1 %collective-permute-start.2 = (bf16[4,6,128]{2,1,0:T(8,128)(2,1)S(1)}, bf16[4,6,128]{2,1,0:T(8,128)(2,1)}, u32[]{:S(2)}, u32[]{:S(2)}) collective-permute-start(bf16[4,6,128]{2,1,0:T(8,128)(2,1)S(1)} %pad_maximum_fusion.1), channel_id=1, source_target_pairs={{0,128},{128,0},{1,129},{129,1},{2,130},{130,2},{3,131},{131,3},{4... | collective-permute-start | bytes 18440 | tf_op jit(solution)/shard_map/ppermute | solution.py:31
  34.1 0.7 fusion.121
  34.7 0.7 copy.90
  36.0 0.9 collective-permute-done.2
  36.8 0.7 select_bitcast_fusion.1
  37.6 0.9 fusion.1
  38.5 0.4 convolution_bitcast_fusion
  38.9 0.8 fusion.128
  40.0 2.0 %constant_dynamic-update-slice_fusion.31 = (bf16[32,10,8,256]{3,2,1,0:T(8,128)(2,1)S(1)}, bf16[1,10,8,256]{3,2,1,0:T(8,128)(2,1)S(1)}, f32[1,10,8,256]{3,2,1,0:T...) fusion(f32[8,256]{1,0:T(8,128)} %get-tuple-element.132, ...), kind=kLoop, calls=%fused_computation.249 | loop fusion | flops 3993599 | bytes 4481104
  42.0 0.7 constant_dynamic-update-slice_fusion.29
  42.8 0.7 constant_dynamic-update-slice_fusion.27
  43.5 0.7 constant_dynamic-update-slice_fusion.25
  44.3 0.7 constant_dynamic-update-slice_fusion.23
  45.5 0.3 copy-done.62
  45.8 0.0 copy-done.60
  45.8 0.0 copy-done.59
  45.9 0.1 constant_dynamic-update-slice_fusion.1
  46.0 0.1 constant_dynamic-update-slice_fusion
  46.1 1.1 %broadcast_multiply_fusion = bf16[32,10,8,256]{3,2,1,0:T(8,128)(2,1)} fusion(bf16[32,10,8,256]{3,2,1,0:T(8,128)(2,1)S(1)} %constant_dynamic-update-slice_fusion, bf16[8,256]{1,0:T(8,128)(2,1)S(1)} %copy-done.71), kind=kLoop, calls=%fused_computation.5 | loop fusion | flops 655360 | bytes 2625536 | tf_op jit(solution)/shard_map/mul | solution.py:151
  47.2 7.7 %all-to-all-start = ((bf16[32,10,8,256]{3,2,1,0:T(8,128)(2,1)}), bf16[32,10,8,256]{3,2,1,0:T(8,128)(2,1)}, u32[]{:S(2)}, u32[]{:S(2)}) async-start(bf16[32,10,8,256]{3,2,1,0:T(8,128)(2,1)} %broadcast_multiply_fusion), calls=%async_computation | async-start | bytes 2621440 | tf_op jit(solution)/shard_map/all_to_all | solution.py:154
  54.9 2.4 %fusion.116 = f32[8,256]{1,0:T(8,128)} fusion(f32[8,256]{1,0:T(8,128)S(1)} %get-tuple-element.80, f32[8,256]{1,0:T(8,128)S(1)} %get-tuple-element.124, f32[8,256]{1,0:T(8,128)S(1)} %bitcast.599, f32[8,256]{1,0:T(8,128)S(1)} %bitcast.603, f32[8,256]{1,0:T(8,128)S(1)} %bitcast.611, f32[8,256]{1,0:T(8,128)} %bitcast.658, f32[8,256]{1,0:T(8,128)} %bitcast.654, ...), kind=kLoop, calls=%fused_computation.217 | loop fusion | flops 2762752 | bytes 1859704 | tf_op jit(solution)/shard_map/reduce_sum | solution.py:149
  57.3 23.7 %psum.7 = f32[8,256]{1,0:T(8,128)S(1)} all-reduce(f32[8,256]{1,0:T(8,128)} %fusion.116), channel_id=1, replica_groups=mesh['sec'=2,'lat'=8,'lon'=16] {'sec'}, use_global_device_ids=true, to_apply=%region_1.2 | all-reduce | flops 2048 | bytes 16384 | tf_op jit(solution)/shard_map/psum | solution.py:150
  81.0 1.3 %compare_select_fusion = f32[8,256]{1,0:T(8,128)} fusion(f32[8,256]{1,0:T(8,128)S(1)} %psum.7, s32[256]{0:T(256)} %copy-done.72, s32[8]{0:T(128)} %param.16), kind=kLoop, calls=%fused_computation.256 | loop fusion | flops 4096 | bytes 17440 | tf_op jit(solution)/shard_map/mul | solution.py:150
  82.4 5.5 %all-to-all-done = bf16[32,10,8,256]{3,2,1,0:T(8,128)(2,1)} async-done(((bf16[32,10,8,256]{3,2,1,0:T(8,128)(2,1)}), bf16[32,10,8,256]{3,2,1,0:T(8,128)(2,1)}, u32[]{:S(2)}, u32[]{:S(2)}) %all-to-all-start) | async-done | bytes 1310752 | tf_op jit(solution)/shard_map/all_to_all | solution.py:154
  87.9 1.4 %copy.94 = bf16[16,2,10,8,256]{4,3,0,2,1:T(8,128)(2,1)S(1)} copy(bf16[16,2,10,8,256]{4,3,2,1,0:T(8,128)(2,1)} %bitcast.109) | data formatting | bytes 2621440 | tf_op jit(solution)/shard_map/all_to_all | solution.py:154
  89.4 8.9 %fusion.190 = f32[2,10,8,2,1280]{4,2,3,1,0:T(8,128)S(1)} fusion(bf16[2,10,8,4096,1]{3,2,4,1,0:T(8,128)(2,1)S(1)} %bitcast.594, bf16[4096,2,1280,1,1]{2,0,1,4,3:T(8,128)(2,1)} %constant.42), kind=kOutput, calls=%fused_computation.419 | convolution fusion | flops 3355443200 | bytes 23920640 | tf_op jit(solution)/shard_map/lbrm,mck->lbrck/dot_general | solution.py:108
  98.2 8.9 %fusion = f32[2,10,8,2,1280]{4,2,3,1,0:T(8,128)S(1)} fusion(f32[2,10,8,2,1280]{4,2,3,1,0:T(8,128)S(1)} %fusion.190, bf16[2,10,8,4096,1]{3,2,4,1,0:T(8,128)(2,1)S(1)} %bitcast.595, bf16[4096,2,1280,1,1]{2,0,1,4,3:T(8,128)(2,1)} %constant.43), kind=kOutput, calls=%fused_computation.1 | convolution fusion | flops 3356262400 | bytes 25559040 | tf_op jit(solution)/shard_map/lbrm,mck->lbrck/dot_general | solution.py:111
  107.1 2.0 %copy.95 = f32[2,10,8,2,1280]{4,3,2,1,0:T(2,128)} copy(f32[2,10,8,2,1280]{4,2,3,1,0:T(8,128)S(1)} %fusion) | data formatting | bytes 3276800
  (188 shorter events, 0.6 us)
Async XLA Ops:
  0.6 37.8 %copy-start = (bf16[8,4,128,256]{3,2,1,0:T(8,128)(2,1)S(1)}, bf16[8,4,128,256]{3,2,1,0:T(8,128)(2,1)}, u32[]{:S(2)}) copy-start(bf16[8,4,128,256]{3,2,1,0:T(8,128)(2,1)} %param.14) | copy-start | bytes 6291460
  0.6 30.9 %copy-start.2 = (f32[32,8,256]{2,1,0:T(8,128)S(1)}, f32[32,8,256]{2,1,0:T(8,128)}, u32[]{:S(2)}) copy-start(f32[32,8,256]{2,1,0:T(8,128)} %param.19) | copy-start | bytes 786436
  0.7 33.4 %copy-start.77 = (s32[8]{0:T(128)S(1)}, s32[8]{0:T(128)}, u32[]{:S(2)}) copy-start(s32[8]{0:T(128)} %param.16) | copy-start | bytes 100
  0.7 34.1 %copy-start.78 = (s32[8,1,4]{0,2,1:T(4,128)S(1)}, s32[8,1,4]{0,2,1:T(4,128)}, u32[]{:S(2)}) copy-start(s32[8,1,4]{0,2,1:T(4,128)} %param.15) | copy-start | bytes 388
  2.2 33.2 %copy-start.70 = (bf16[4,2,128]{2,1,0:T(2,128)(2,1)}, bf16[4,2,128]{2,1,0:T(2,128)(2,1)S(1)}, u32[]{:S(2)}) copy-start(bf16[4,2,128]{2,1,0:T(2,128)(2,1)S(1)} %bitcast_multiply_fusion) | copy-start | bytes 6148
  2.2 30.7 %collective-permute-start.1 = (bf16[4,2,128]{2,1,0:T(2,128)(2,1)S(1)}, bf16[4,2,128]{2,1,0:T(2,128)(2,1)S(1)}, u32[]{:S(2)}, u32[]{:S(2)}) collective-permute-start(bf16[4,2,128]{2,1,0:T(2,128)(2,1)S(1)} %bitcast_multiply_fusion), channel_id=1, source_target_pairs={{1,0},{2,1},{3,2},{4,3},{5,4},{6,5},{7,6},{8,7},{9,8},{10,9},{11,1... | collective-permute-start | bytes 6152 | tf_op jit(solution)/shard_map/ppermute | solution.py:23
  10.7 22.2 %collective-permute-start = (bf16[4,2,128]{2,1,0:T(2,128)(2,1)S(1)}, bf16[4,2,128]{2,1,0:T(2,128)(2,1)S(1)}, u32[]{:S(2)}, u32[]{:S(2)}) collective-permute-start(bf16[4,2,128]{2,1,0:T(2,128)(2,1)S(1)} %bitcast_multiply_fusion), channel_id=1, source_target_pairs={{0,1},{1,2},{2,3},{3,4},{4,5},{5,6},{6,7},{7,8},{8,9},{9,10},{10,1... | collective-permute-start | bytes 6152 | tf_op jit(solution)/shard_map/ppermute | solution.py:20
  17.5 17.9 %copy-start.3 = (f32[1,8,256]{2,1,0:T(8,128)}, f32[1,8,256]{2,1,0:T(8,128)S(1)}, u32[]{:S(2)}) copy-start(f32[1,8,256]{2,1,0:T(8,128)S(1)} %get-tuple-element.52) | copy-start | bytes 24580
  18.9 16.5 %copy-start.7 = (f32[1,8,256]{2,1,0:T(8,128)}, f32[1,8,256]{2,1,0:T(8,128)S(1)}, u32[]{:S(2)}) copy-start(f32[1,8,256]{2,1,0:T(8,128)S(1)} %get-tuple-element.55) | copy-start | bytes 24580
  20.5 8.2 %copy-start.9 = (f32[1,8,256]{2,1,0:T(8,128)}, f32[1,8,256]{2,1,0:T(8,128)S(1)}, u32[]{:S(2)}) copy-start(f32[1,8,256]{2,1,0:T(8,128)S(1)} %get-tuple-element.57) | copy-start | bytes 24580
  20.5 14.9 %copy-start.11 = (f32[1,8,256]{2,1,0:T(8,128)}, f32[1,8,256]{2,1,0:T(8,128)S(1)}, u32[]{:S(2)}) copy-start(f32[1,8,256]{2,1,0:T(8,128)S(1)} %get-tuple-element.58) | copy-start | bytes 24580
  21.9 8.2 %copy-start.13 = (f32[1,8,256]{2,1,0:T(8,128)}, f32[1,8,256]{2,1,0:T(8,128)S(1)}, u32[]{:S(2)}) copy-start(f32[1,8,256]{2,1,0:T(8,128)S(1)} %get-tuple-element.60) | copy-start | bytes 24580
  21.9 13.6 %copy-start.15 = (f32[1,8,256]{2,1,0:T(8,128)}, f32[1,8,256]{2,1,0:T(8,128)S(1)}, u32[]{:S(2)}) copy-start(f32[1,8,256]{2,1,0:T(8,128)S(1)} %get-tuple-element.61) | copy-start | bytes 24580
  23.2 6.8 %copy-start.17 = (f32[1,8,256]{2,1,0:T(8,128)}, f32[1,8,256]{2,1,0:T(8,128)S(1)}, u32[]{:S(2)}) copy-start(f32[1,8,256]{2,1,0:T(8,128)S(1)} %get-tuple-element.63) | copy-start | bytes 24580
  23.2 12.2 %copy-start.19 = (f32[1,8,256]{2,1,0:T(8,128)}, f32[1,8,256]{2,1,0:T(8,128)S(1)}, u32[]{:S(2)}) copy-start(f32[1,8,256]{2,1,0:T(8,128)S(1)} %get-tuple-element.64) | copy-start | bytes 24580
  24.6 5.5 %copy-start.21 = (f32[1,8,256]{2,1,0:T(8,128)}, f32[1,8,256]{2,1,0:T(8,128)S(1)}, u32[]{:S(2)}) copy-start(f32[1,8,256]{2,1,0:T(8,128)S(1)} %get-tuple-element.66) | copy-start | bytes 24580
  24.6 10.8 %copy-start.23 = (f32[1,8,256]{2,1,0:T(8,128)}, f32[1,8,256]{2,1,0:T(8,128)S(1)}, u32[]{:S(2)}) copy-start(f32[1,8,256]{2,1,0:T(8,128)S(1)} %get-tuple-element.67) | copy-start | bytes 24580
  26.0 9.5 %copy-start.25 = (f32[1,8,256]{2,1,0:T(8,128)}, f32[1,8,256]{2,1,0:T(8,128)S(1)}, u32[]{:S(2)}) copy-start(f32[1,8,256]{2,1,0:T(8,128)S(1)} %get-tuple-element.69) | copy-start | bytes 24580
  26.0 9.5 %copy-start.27 = (f32[1,8,256]{2,1,0:T(8,128)}, f32[1,8,256]{2,1,0:T(8,128)S(1)}, u32[]{:S(2)}) copy-start(f32[1,8,256]{2,1,0:T(8,128)S(1)} %get-tuple-element.70) | copy-start | bytes 24580
  27.3 8.2 %copy-start.29 = (f32[1,8,256]{2,1,0:T(8,128)}, f32[1,8,256]{2,1,0:T(8,128)S(1)}, u32[]{:S(2)}) copy-start(f32[1,8,256]{2,1,0:T(8,128)S(1)} %get-tuple-element.72) | copy-start | bytes 24580
  27.3 8.2 %copy-start.31 = (f32[1,8,256]{2,1,0:T(8,128)}, f32[1,8,256]{2,1,0:T(8,128)S(1)}, u32[]{:S(2)}) copy-start(f32[1,8,256]{2,1,0:T(8,128)S(1)} %get-tuple-element.73) | copy-start | bytes 24580
  28.7 6.8 %copy-start.33 = (f32[1,8,256]{2,1,0:T(8,128)}, f32[1,8,256]{2,1,0:T(8,128)S(1)}, u32[]{:S(2)}) copy-start(f32[1,8,256]{2,1,0:T(8,128)S(1)} %get-tuple-element.75) | copy-start | bytes 24580
  28.7 6.8 %copy-start.35 = (f32[1,8,256]{2,1,0:T(8,128)}, f32[1,8,256]{2,1,0:T(8,128)S(1)}, u32[]{:S(2)}) copy-start(f32[1,8,256]{2,1,0:T(8,128)S(1)} %get-tuple-element.76) | copy-start | bytes 24580
  30.0 5.5 %copy-start.37 = (f32[1,8,256]{2,1,0:T(8,128)}, f32[1,8,256]{2,1,0:T(8,128)S(1)}, u32[]{:S(2)}) copy-start(f32[1,8,256]{2,1,0:T(8,128)S(1)} %get-tuple-element.79) | copy-start | bytes 24580
  33.0 3.8 %collective-permute-start.2 = (bf16[4,6,128]{2,1,0:T(8,128)(2,1)S(1)}, bf16[4,6,128]{2,1,0:T(8,128)(2,1)}, u32[]{:S(2)}, u32[]{:S(2)}) collective-permute-start(bf16[4,6,128]{2,1,0:T(8,128)(2,1)S(1)} %pad_maximum_fusion.1), channel_id=1, source_target_pairs={{0,128},{128,0},{1,129},{129,1},{2,130},{130,2},{3,131},{131,3},{4... | collective-permute-start | bytes 18440 | tf_op jit(solution)/shard_map/ppermute | solution.py:31
  35.6 4.1 %copy-start.1 = (bf16[32,10,8,256]{3,2,1,0:T(8,128)(2,1)S(1)}, bf16[32,10,8,256]{3,2,1,0:T(8,128)(2,1)}, u32[]{:S(2)}) copy-start(bf16[32,10,8,256]{3,2,1,0:T(8,128)(2,1)} %param.18) | copy-start | bytes 3932164
  35.6 4.1 %copy-start.4 = (f32[1,8,256]{2,1,0:T(8,128)S(1)}, f32[1,8,256]{2,1,0:T(8,128)}, u32[]{:S(2)}) copy-start(f32[1,8,256]{2,1,0:T(8,128)} %copy-done.3) | copy-start | bytes 24580
  35.6 4.1 %copy-start.6 = (f32[1,8,256]{2,1,0:T(8,128)S(1)}, f32[1,8,256]{2,1,0:T(8,128)}, u32[]{:S(2)}) copy-start(f32[1,8,256]{2,1,0:T(8,128)} %copy-done.5) | copy-start | bytes 24580
  35.6 4.1 %copy-start.8 = (f32[1,8,256]{2,1,0:T(8,128)S(1)}, f32[1,8,256]{2,1,0:T(8,128)}, u32[]{:S(2)}) copy-start(f32[1,8,256]{2,1,0:T(8,128)} %copy-done.7) | copy-start | bytes 24580
  35.6 4.1 %copy-start.10 = (f32[1,8,256]{2,1,0:T(8,128)S(1)}, f32[1,8,256]{2,1,0:T(8,128)}, u32[]{:S(2)}) copy-start(f32[1,8,256]{2,1,0:T(8,128)} %copy-done.9) | copy-start | bytes 24580
  35.6 4.1 %copy-start.12 = (f32[1,8,256]{2,1,0:T(8,128)S(1)}, f32[1,8,256]{2,1,0:T(8,128)}, u32[]{:S(2)}) copy-start(f32[1,8,256]{2,1,0:T(8,128)} %copy-done.11) | copy-start | bytes 24580
  35.6 4.1 %copy-start.14 = (f32[1,8,256]{2,1,0:T(8,128)S(1)}, f32[1,8,256]{2,1,0:T(8,128)}, u32[]{:S(2)}) copy-start(f32[1,8,256]{2,1,0:T(8,128)} %copy-done.13) | copy-start | bytes 24580
  35.6 4.1 %copy-start.16 = (f32[1,8,256]{2,1,0:T(8,128)S(1)}, f32[1,8,256]{2,1,0:T(8,128)}, u32[]{:S(2)}) copy-start(f32[1,8,256]{2,1,0:T(8,128)} %copy-done.15) | copy-start | bytes 24580
  35.6 4.1 %copy-start.18 = (f32[1,8,256]{2,1,0:T(8,128)S(1)}, f32[1,8,256]{2,1,0:T(8,128)}, u32[]{:S(2)}) copy-start(f32[1,8,256]{2,1,0:T(8,128)} %copy-done.17) | copy-start | bytes 24580
  35.7 4.1 %copy-start.20 = (f32[1,8,256]{2,1,0:T(8,128)S(1)}, f32[1,8,256]{2,1,0:T(8,128)}, u32[]{:S(2)}) copy-start(f32[1,8,256]{2,1,0:T(8,128)} %copy-done.19) | copy-start | bytes 24580
  35.7 4.1 %copy-start.22 = (f32[1,8,256]{2,1,0:T(8,128)S(1)}, f32[1,8,256]{2,1,0:T(8,128)}, u32[]{:S(2)}) copy-start(f32[1,8,256]{2,1,0:T(8,128)} %copy-done.21) | copy-start | bytes 24580
  35.7 4.1 %copy-start.24 = (f32[1,8,256]{2,1,0:T(8,128)S(1)}, f32[1,8,256]{2,1,0:T(8,128)}, u32[]{:S(2)}) copy-start(f32[1,8,256]{2,1,0:T(8,128)} %copy-done.23) | copy-start | bytes 24580
  35.7 4.1 %copy-start.26 = (f32[1,8,256]{2,1,0:T(8,128)S(1)}, f32[1,8,256]{2,1,0:T(8,128)}, u32[]{:S(2)}) copy-start(f32[1,8,256]{2,1,0:T(8,128)} %copy-done.25) | copy-start | bytes 24580
  35.7 4.1 %copy-start.28 = (f32[1,8,256]{2,1,0:T(8,128)S(1)}, f32[1,8,256]{2,1,0:T(8,128)}, u32[]{:S(2)}) copy-start(f32[1,8,256]{2,1,0:T(8,128)} %copy-done.27) | copy-start | bytes 24580
  35.7 4.1 %copy-start.30 = (f32[1,8,256]{2,1,0:T(8,128)S(1)}, f32[1,8,256]{2,1,0:T(8,128)}, u32[]{:S(2)}) copy-start(f32[1,8,256]{2,1,0:T(8,128)} %copy-done.29) | copy-start | bytes 24580
  35.7 4.1 %copy-start.32 = (f32[1,8,256]{2,1,0:T(8,128)S(1)}, f32[1,8,256]{2,1,0:T(8,128)}, u32[]{:S(2)}) copy-start(f32[1,8,256]{2,1,0:T(8,128)} %copy-done.31) | copy-start | bytes 24580
  35.7 4.1 %copy-start.34 = (f32[1,8,256]{2,1,0:T(8,128)S(1)}, f32[1,8,256]{2,1,0:T(8,128)}, u32[]{:S(2)}) copy-start(f32[1,8,256]{2,1,0:T(8,128)} %copy-done.33) | copy-start | bytes 24580
  35.7 4.1 %copy-start.36 = (f32[1,8,256]{2,1,0:T(8,128)S(1)}, f32[1,8,256]{2,1,0:T(8,128)}, u32[]{:S(2)}) copy-start(f32[1,8,256]{2,1,0:T(8,128)} %copy-done.35) | copy-start | bytes 24580
  35.7 4.1 %copy-start.38 = (f32[1,8,256]{2,1,0:T(8,128)S(1)}, f32[1,8,256]{2,1,0:T(8,128)}, u32[]{:S(2)}) copy-start(f32[1,8,256]{2,1,0:T(8,128)} %copy-done.37) | copy-start | bytes 24580
  35.8 4.1 %copy-start.39 = (f32[8,256]{1,0:T(8,128)S(1)}, f32[8,256]{1,0:T(8,128)}, u32[]{:S(2)}) copy-start(f32[8,256]{1,0:T(8,128)} %get-tuple-element.125) | copy-start | bytes 24580
  35.8 4.1 %copy-start.40 = (f32[8,256]{1,0:T(8,128)S(1)}, f32[8,256]{1,0:T(8,128)}, u32[]{:S(2)}) copy-start(f32[8,256]{1,0:T(8,128)} %get-tuple-element.127) | copy-start | bytes 24580
  35.8 4.1 %copy-start.41 = (f32[8,256]{1,0:T(8,128)S(1)}, f32[8,256]{1,0:T(8,128)}, u32[]{:S(2)}) copy-start(f32[8,256]{1,0:T(8,128)} %get-tuple-element.129) | copy-start | bytes 24580
  47.2 40.7 %all-to-all-start = ((bf16[32,10,8,256]{3,2,1,0:T(8,128)(2,1)}), bf16[32,10,8,256]{3,2,1,0:T(8,128)(2,1)}, u32[]{:S(2)}, u32[]{:S(2)}) async-start(bf16[32,10,8,256]{3,2,1,0:T(8,128)(2,1)} %broadcast_multiply_fusion), calls=%async_computation | async-start | bytes 2621440 | tf_op jit(solution)/shard_map/all_to_all | solution.py:154
  (35 other events, 104.2 us)
where the time goes:
time: 111 us; the launch traced here: 109 us
  other arithmetic  36 us (32%)
  blocking collectives  23.7 us (21%)
  matrix products  19 us (17%)
  starting transfers between devices  17.3 us (16%)
  waiting for transfers between devices  6.4 us (6%)
  local copies, waits for them, and re-layouts  4.79 us (4%)
  between operations  1.96 us (2%)
    psum x1, blocking collectives, on_device(): salt_flux = lax.psum(partial_salt, 'sec') * valid  23.7 us
    mul x16, other arithmetic, solve_columns(): carried = scaled[level] + ratios[level] * carried  20.5 us
    dot_general x1, matrix products, transform(): jnp.einsum('lbrm,mck->lbrck', block_rows, table_low, preferred_element_ty...  8.87 us
    dot_general x1, matrix products, transform(): jnp.einsum('lbrm,mck->lbrck', block_rows, table_high, preferred_element_t...  8.86 us
    ppermute x1, starting transfers between devices, padded(): lax.ppermute(lax.slice_in_dim(block, 0, width, axis=dim), axis, backward)  8.5 us
    all_to_all x1, starting transfers between devices, on_device(): lax.all_to_all(spectral_in, 'lon', split_axis=0, concat_axis=3, tiled=True)  7.67 us
    all_to_all x1, waiting for transfers between devices, on_device(): lax.all_to_all(spectral_in, 'lon', split_axis=0, concat_axis=3, tiled=True)  5.54 us
    unnamed x30, other arithmetic  5.18 us
  transfers between devices with their start and end apart: 4, of which 2 were waited for; matrix products, arithmetic and copies ran while one was open for 25% of the time, Pallas kernels for 0%

commit v1 on v0

v1 whole, which is shorter than its diff:
```python
import functools
import math

import jax
import jax.numpy as jnp
import numpy as np
from jax import lax
from jax.experimental import pallas as pl
from jax.experimental.pallas import tpu as pltpu
from jax.sharding import PartitionSpec as P

M = 4096
K = 1280
LEV = 32
TILES = 16
PTS = 256
NBD = 10
ROWS = 8
CHUNK = 2
NCHUNK = NBD // CHUNK
MESH = pl.DeviceIdType.MESH


def mix_kernel(
    ocean_ref,
    sea_ref,
    src_ref,
    points_ref,
    emit_ref,
    settle_ref,
    mass_ref,
    wind_hbm,
    weights_hbm,
    conc_hbm,
    kdiff_hbm,
    recv_hbm,
    salt_ref,
    wind_ref,
    weights_ref,
    conc_ref,
    kdiff_ref,
    near_ref,
    lhs_ref,
    fields_ref,
    ratio_ref,
    scaled_ref,
    out_ref,
    part_ref,
    other_ref,
    local_sem,
    own_sem,
    near_send,
    near_recv,
    salt_send,
    salt_recv,
    a2a_send,
    a2a_recv,
):
    sec = lax.axis_index("sec")
    lat = lax.axis_index("lat")
    lon = lax.axis_index("lon")

    barrier = pltpu.get_barrier_semaphore()
    for step in range(1, TILES):
        peer = lax.rem(lon + step, TILES)
        pl.semaphore_signal(barrier, inc=1, device_id=(sec, lat, peer), device_id_type=MESH)
    for shift in (-1, 0, 1):
        peer = lax.rem(lon + shift + TILES, TILES)
        pl.semaphore_signal(barrier, inc=1, device_id=(1 - sec, lat, peer), device_id_type=MESH)

    loads = [
        pltpu.make_async_copy(kdiff_hbm, kdiff_ref, local_sem.at[0]),
        pltpu.make_async_copy(conc_hbm, conc_ref, local_sem.at[1]),
        pltpu.make_async_copy(weights_hbm, weights_ref, local_sem.at[2]),
        pltpu.make_async_copy(wind_hbm, wind_ref, local_sem.at[3]),
    ]
    for load in loads:
        load.start()

    own_slot = sec * 6 + 2
    ocean = ocean_ref[...].astype(jnp.float32)
    for block in range(2):
        near_ref[own_slot + block] = jnp.zeros((8, 128), jnp.float32)
        sea = sea_ref[0, block].astype(jnp.float32)
        near_ref[own_slot + block, 0:4, :] = ocean[:, block, :] * sea

    pl.semaphore_wait(barrier, TILES - 1 + 3)

    near_copies = []
    index = 0
    for same_sec in (True, False):
        for shift in (-1, 0, 1):
            if same_sec and shift == 0:
                continue
            peer = lax.rem(lon + shift + TILES, TILES)
            to_sec = sec if same_sec else 1 - sec
            copy = pltpu.make_async_remote_copy(
                src_ref=near_ref.at[pl.ds(own_slot, 2)],
                dst_ref=near_ref.at[pl.ds(sec * 6 + (1 - shift) * 2, 2)],
                send_sem=near_send.at[index],
                recv_sem=near_recv.at[index],
                device_id=(to_sec, lat, peer),
                device_id_type=MESH,
            )
            copy.start()
            near_copies.append(copy)
            index += 1

    loads[0].wait()
    loads[1].wait()

    def eliminate(level, carried):
        ratio_prev, scaled_prev = carried
        here = kdiff_ref[level]
        below = kdiff_ref[level + 1]
        inverse = 1.0 / (1.0 + here + below - here * ratio_prev)
        ratio_now = below * inverse
        ratio_ref[level] = ratio_now
        scaled_now = []
        for b in range(NBD):
            value = (conc_ref[level, b].astype(jnp.float32) + here * scaled_prev[b]) * inverse
            scaled_ref[level, b] = value
            scaled_now.append(value)
        return ratio_now, tuple(scaled_now)

    zero = jnp.zeros((ROWS, PTS), jnp.float32)
    ratio_last, scaled_last = lax.fori_loop(0, LEV - 1, eliminate, (zero, (zero,) * NBD))

    row_ids = lax.broadcasted_iota(jnp.int32, (ROWS, PTS), 0)
    columns = lax.broadcasted_iota(jnp.int32, (ROWS, PTS), 1) + lon * PTS
    limits = jnp.zeros((ROWS, PTS), jnp.int32)
    for r in range(ROWS):
        limits = jnp.where(row_ids == r, points_ref[r], limits)
    valid = (columns < limits).astype(jnp.float32)

    loads[2].wait()
    loads[3].wait()
    for copy in near_copies:
        copy.wait()

    for r in range(ROWS):
        for s in range(4):
            lhs_ref[r, :, s * 128 : (s + 1) * 128] = near_ref[src_ref[0, s, r]]
    for r in range(ROWS):
        fields_ref[r] = jnp.dot(
            lhs_ref[r].astype(jnp.bfloat16),
            weights_ref[r].reshape(512, PTS),
            preferred_element_type=jnp.float32,
        )
    temp = fields_ref[:, 0, :]
    ice = fields_ref[:, 1, :]
    rel_east = wind_ref[0] - 0.5 * fields_ref[:, 2, :]
    rel_north = wind_ref[1] - 0.5 * fields_ref[:, 3, :]
    speed = jnp.sqrt(rel_east * rel_east + rel_north * rel_north + 0.25)
    base = (
        (1.0 - jax.nn.sigmoid(ice))
        * jnp.exp(3.41 * jnp.log(speed))
        * (0.5 + jax.nn.sigmoid(temp))
        * valid
    )

    last_kdiff = kdiff_ref[LEV - 1]
    pivot_part = 1.0 + last_kdiff - last_kdiff * ratio_last
    partial = zero
    for b in range(NBD):
        flux = emit_ref[b] * base
        settle = settle_ref[b]
        value = (
            conc_ref[LEV - 1, b].astype(jnp.float32) + flux + last_kdiff * scaled_last[b]
        ) / (pivot_part + settle)
        scaled_ref[LEV - 1, b] = value
        partial = partial + mass_ref[b] * (flux - settle * value)
    part_ref[...] = partial

    salt_copy = pltpu.make_async_remote_copy(
        src_ref=part_ref,
        dst_ref=other_ref,
        send_sem=salt_send,
        recv_sem=salt_recv,
        device_id=(1 - sec, lat, lon),
        device_id_type=MESH,
    )

    def a2a_copy(chunk, step):
        peer = lax.rem(lon + step, TILES)
        bins = pl.ds(chunk * CHUNK, CHUNK)
        return pltpu.make_async_remote_copy(
            src_ref=out_ref.at[pl.ds(peer * 2, 2), bins],
            dst_ref=recv_hbm.at[lon, :, bins],
            send_sem=a2a_send.at[chunk, step],
            recv_sem=a2a_recv.at[chunk, step],
            device_id=(sec, lat, peer),
            device_id_type=MESH,
        )

    def own_copy(chunk):
        bins = pl.ds(chunk * CHUNK, CHUNK)
        return pltpu.make_async_copy(
            out_ref.at[pl.ds(lon * 2, 2), bins], recv_hbm.at[lon, :, bins], own_sem.at[chunk]
        )

    keep = valid > 0.0
    for chunk in range(NCHUNK):
        first = chunk * CHUNK
        start = tuple(scaled_ref[LEV - 1, first + b] for b in range(CHUNK))
        for b in range(CHUNK):
            out_ref[LEV - 1, first + b] = jnp.where(keep, start[b], 0.0).astype(jnp.bfloat16)

        def substitute(count, carried, first=first):
            level = LEV - 2 - count
            ratio = ratio_ref[level]
            values = []
            for b in range(CHUNK):
                value = scaled_ref[level, first + b] + ratio * carried[b]
                out_ref[level, first + b] = jnp.where(keep, value, 0.0).astype(jnp.bfloat16)
                values.append(value)
            return tuple(values)

        lax.fori_loop(0, LEV - 1, substitute, start)
        if chunk == 0:
            salt_copy.start()

        @pl.loop(1, TILES)
        def _(step, chunk=chunk):
            a2a_copy(chunk, step).start()

        own_copy(chunk).start()

    salt_copy.wait()
    salt_ref[...] = (part_ref[...] + other_ref[...]) * valid

    for chunk in range(NCHUNK):
        own_copy(chunk).wait()

        @pl.loop(1, TILES)
        def _(step, chunk=chunk):
            a2a_copy(chunk, step).wait()


def mix_and_exchange(ocean, sea, src, points, emit, settle, mass, wind, weights, conc, kdiff):
    vmem = pl.BlockSpec(memory_space=pltpu.VMEM)
    smem = pl.BlockSpec(memory_space=pltpu.SMEM)
    anywhere = pl.BlockSpec(memory_space=pl.ANY)
    dma = pltpu.SemaphoreType.DMA
    return pl.pallas_call(
        mix_kernel,
        name="mix_and_exchange",
        out_shape=(
            jax.ShapeDtypeStruct((TILES, 2, NBD, ROWS, PTS), jnp.bfloat16),
            jax.ShapeDtypeStruct((ROWS, PTS), jnp.float32),
        ),
        in_specs=[vmem] + [smem] * 6 + [anywhere] * 4,
        out_specs=(anywhere, vmem),
        scratch_shapes=[
            pltpu.VMEM((2, ROWS, PTS), jnp.float32),
            pltpu.VMEM((ROWS, 4, 128, PTS), jnp.bfloat16),
            pltpu.VMEM((LEV, NBD, ROWS, PTS), jnp.bfloat16),
            pltpu.VMEM((LEV, ROWS, PTS), jnp.float32),
            pltpu.VMEM((12, 8, 128), jnp.float32),
            pltpu.VMEM((ROWS, 8, 512), jnp.float32),
            pltpu.VMEM((ROWS, 8, PTS), jnp.float32),
            pltpu.VMEM((LEV, ROWS, PTS), jnp.float32),
            pltpu.VMEM((LEV, NBD, ROWS, PTS), jnp.float32),
            pltpu.VMEM((LEV, NBD, ROWS, PTS), jnp.bfloat16),
            pltpu.VMEM((ROWS, PTS), jnp.float32),
            pltpu.VMEM((ROWS, PTS), jnp.float32),
            dma((4,)),
            dma((NCHUNK,)),
            dma((5,)),
            dma((5,)),
            dma,
            dma,
            dma((NCHUNK, TILES)),
            dma((NCHUNK, TILES)),
        ],
        compiler_params=pltpu.CompilerParams(collective_id=0, has_side_effects=True),
    )(ocean, sea, src, points, emit, settle, mass, wind, weights, conc, kdiff)


def twiddles():
    phase = np.arange(TILES)[:, None] * np.arange(PTS)[None, :] * (2.0 * np.pi / M)
    parts = np.stack([np.cos(phase), np.sin(phase)], axis=1) * (1.0 / math.sqrt(M))
    return parts.astype(np.float32)


def row_table():
    column = np.arange(256)
    combo = (column // 128) * 16 + column % 16
    ka = 8 * (combo // 2) + (column % 128) // 16
    phase = np.arange(PTS)[:, None] * ka[None, :] % PTS * (2.0 * np.pi / PTS)
    cos, sin = np.cos(phase), np.sin(phase)
    is_cos = (combo % 2 == 0)[None, :]
    upper = np.where(is_cos, cos, -sin)
    lower = np.where(is_cos, -sin, -cos)
    table = np.concatenate([upper, lower], axis=0) * (combo < 20)[None, :]
    return table.astype(np.float32)


def real_dft16(x):
    c1, c2, c3 = math.cos(math.pi / 8), math.cos(math.pi / 4), math.cos(3 * math.pi / 8)
    s = [x[i] + x[i + 8] for i in range(8)]
    d = [x[i] - x[i + 8] for i in range(8)]
    a = [s[i] + s[i + 4] for i in range(4)]
    b = [s[i] - s[i + 4] for i in range(4)]
    out = [None] * 9
    a02, a13 = a[0] + a[2], a[1] + a[3]
    out[0] = (a02 + a13, None)
    out[8] = (a02 - a13, None)
    out[4] = (a[0] - a[2], a[1] - a[3])
    bm, bp = (b[1] - b[3]) * c2, (b[1] + b[3]) * c2
    out[2] = (b[0] + bm, bp + b[2])
    out[6] = (b[0] - bm, bp - b[2])
    e1, e2, e3 = d[1] - d[7], (d[2] - d[6]) * c2, d[3] - d[5]
    f1, f2, f3 = d[1] + d[7], (d[2] + d[6]) * c2, d[3] + d[5]
    p, q = d[0] + e2, d[0] - e2
    u, v = e1 * c1 + e3 * c3, e1 * c3 - e3 * c1
    g, h = f1 * c3 + f3 * c1, f1 * c1 - f3 * c3
    m, n = f2 + d[4], f2 - d[4]
    out[1] = (p + u, g + m)
    out[7] = (p - u, g - m)
    out[3] = (q + v, h + n)
    out[5] = (q - v, h - n)
    return out


def transform_kernel(x_ref, twiddle_ref, table_ref, salt_in_ref, y_ref, salt_ref, z_ref, o_ref):
    salt_ref[...] = salt_in_ref[...]
    for half in range(2):
        lanes = slice(half * 128, (half + 1) * 128)
        x = [
            x_ref[tile, 0, :, :, lanes].astype(jnp.float32).reshape(16, 128)
            for tile in range(TILES)
        ]
        coefficients = real_dft16(x)
        for kb in range(TILES):
            re, im = coefficients[min(kb, TILES - kb)]
            cos = twiddle_ref[kb, 0:1, lanes]
            sin = twiddle_ref[kb, 1:2, lanes]
            if im is None:
                real, minus = re * cos, re * sin
            elif kb < 8:
                real, minus = re * cos - im * sin, re * sin + im * cos
            else:
                real, minus = re * cos + im * sin, re * sin - im * cos
            z_ref[kb, :, half * 128 : (half + 1) * 128] = real.astype(jnp.bfloat16)
            z_ref[kb, :, PTS + half * 128 : PTS + (half + 1) * 128] = minus.astype(jnp.bfloat16)
    o_ref[...] = jnp.dot(
        z_ref[...].reshape(TILES * 16, 2 * PTS), table_ref[...], preferred_element_type=jnp.float32
    ).reshape(TILES, 16, 256)
    lane = lax.broadcasted_iota(jnp.int32, (8, 128), 1)
    for group in range(2):
        for q in range(2):
            combos = 16 if q == 0 else 4
            arrays = {
                kb: pltpu.roll(
                    o_ref[kb, group * 8 : (group + 1) * 8, q * 128 : (q + 1) * 128], kb, axis=1
                )
                for kb in range(TILES)
            }
            wanted = {(-t) % TILES for t in range(combos)}
            needs = [wanted]
            for bit in (0, 1, 2):
                wanted = wanted | {(j + (1 << bit)) % TILES for j in wanted}
                needs.append(wanted)
            for bit in (3, 2, 1, 0):
                taken = (lane & (1 << bit)) != 0
                arrays = {
                    j: jnp.where(taken, arrays[(j + (1 << bit)) % TILES], arrays[j])
                    for j in needs[bit]
                }
            for t in range(combos):
                value = arrays[(-t) % TILES]
                if t:
                    value = pltpu.roll(value, 128 - t, axis=1)
                c, part = divmod(q * 16 + t, 2)
                y_ref[0, group, :, part, c * 128 : (c + 1) * 128] = value


def transform(received, salt):
    whole = lambda *shape: pl.BlockSpec(shape, lambda i, j: (0,) * len(shape))
    return pl.pallas_call(
        transform_kernel,
        name="transform",
        grid=(2, NBD // 2),
        out_shape=(
            jax.ShapeDtypeStruct((2, NBD, ROWS, 2, K), jnp.float32),
            jax.ShapeDtypeStruct((ROWS, PTS), jnp.float32),
        ),
        in_specs=[
            pl.BlockSpec((TILES, 1, 2, ROWS, PTS), lambda i, j: (0, i, j, 0, 0)),
            whole(TILES, 2, PTS),
            whole(2 * PTS, 256),
            whole(ROWS, PTS),
        ],
        out_specs=(
            pl.BlockSpec((1, 2, ROWS, 2, K), lambda i, j: (i, j, 0, 0, 0)),
            whole(ROWS, PTS),
        ),
        scratch_shapes=[
            pltpu.VMEM((TILES, 16, 2 * PTS), jnp.bfloat16),
            pltpu.VMEM((TILES, 16, 256), jnp.float32),
        ],
    )(received, jnp.asarray(twiddles()), jnp.asarray(row_table()).astype(jnp.bfloat16), salt)


def on_device(
    ocean_state,
    sea_tiles,
    regrid_weights,
    regrid_src,
    row_points,
    wind,
    conc,
    kdiff,
    bin_emit,
    bin_settle,
    bin_mass,
):
    received, salt = mix_and_exchange(
        ocean_state.reshape(4, 2, 128),
        sea_tiles.reshape(1, 2),
        jnp.transpose(regrid_src, (1, 2, 0)),
        row_points,
        bin_emit,
        bin_settle,
        bin_mass,
        wind,
        regrid_weights,
        conc,
        kdiff,
    )
    return transform(received, salt)


def solution(mesh):
    return jax.shard_map(
        on_device,
        mesh=mesh,
        in_specs=(
            P(None, "sec", "lat", "lon", None),
            P("sec", "lat", "lon"),
            P("lat", None, None, "lon"),
            P("lat", "lon", None),
            P("lat"),
            P(None, "lat", "lon"),
            P(None, "sec", "lat", "lon"),
            P(None, "lat", "lon"),
            P("sec"),
            P("sec"),
            P("sec"),
        ),
        out_specs=(P("lon", "sec", "lat", None, None), P("lat", "lon")),
        check_vma=False,
    )
```

time: 111 us -> 57.4 us (0.52); the launches traced: 109 us -> 57.1 us
  Pallas kernels: 0 us -> 56.5 us
  other arithmetic: 36 us -> 0 us
  blocking collectives: 23.7 us -> 0 us
  matrix products: 19 us -> 0 us
  starting transfers between devices: 17.3 us -> 0 us
  waiting for transfers between devices: 6.4 us -> 0 us
  local copies, waits for them, and re-layouts: 4.79 us -> 0 us
  between operations: 1.96 us -> 0.64 us
    pallas_call x0 -> x2, Pallas kernels: none -> 56.5 us  [the longest x1 47.6 us: mix_and_exchange(): pl.pallas_call(mix_kernel, name='mix_and_exchange', out_shape=(jax.ShapeD...]
    mul x20 -> x0, other arithmetic: 24.6 us -> none  [the longest x16 20.5 us: solve_columns(): carried = scaled[level] + ratios[level] * carried]
    psum x1 -> x0, blocking collectives: 23.7 us -> none  [on_device(): salt_flux = lax.psum(partial_salt, 'sec') * valid]
    dot_general x4 -> x0, matrix products: 19 us -> none  [the longest x1 8.87 us: transform(): jnp.einsum('lbrm,mck->lbrck', block_rows, table_low, preferred_element_ty...]
    ppermute x3 -> x0, starting transfers between devices: 9.6 us -> none  [the longest x1 8.5 us: padded(): lax.ppermute(lax.slice_in_dim(block, 0, width, axis=dim), axis, backward)]
    all_to_all x1 -> x0, starting transfers between devices: 7.67 us -> none  [on_device(): lax.all_to_all(spectral_in, 'lon', split_axis=0, concat_axis=3, tiled=True)]
    all_to_all x1 -> x0, waiting for transfers between devices: 5.54 us -> none  [on_device(): lax.all_to_all(spectral_in, 'lon', split_axis=0, concat_axis=3, tiled=True)]
    unnamed x30 -> x0, other arithmetic: 5.18 us -> none
  transfers between devices with their start and end apart: 4 -> 0, of which waited for: 2 -> 0; matrix products, arithmetic and copies ran while one was open for 25% -> 0% of each run, Pallas kernels for 0% -> 0%
where the time goes in v1:
time: 57.4 us; the launch traced here: 57.1 us
  Pallas kernels  56.5 us (98%)
  between operations  0.64 us (1%)
    pallas_call x1, Pallas kernels, mix_and_exchange(): pl.pallas_call(mix_kernel, name='mix_and_exchange', out_shape=(jax.ShapeD...  47.6 us
    pallas_call x1, Pallas kernels, transform(): pl.pallas_call(transform_kernel, name='transform', grid=(2, NBD // 2), ou...  8.88 us

profile of v1, /device:TPU:16, one launch (start us, length us, event | category | flops | bytes accessed | tf_op | source)
XLA Modules:
  0.0 57.1 jit_solution(2964299534792866504)
XLA Ops:
  0.6 47.6 %mix_and_exchange.1 = (bf16[16,2,10,8,256]{4,3,2,1,0:T(8,128)(2,1)}, f32[8,256]{1,0:T(8,128)}) custom-call(bf16[4,2,128]{2,1,0:T(2,128)(2,1)} %bitcast.3, s32[1,2]{1,0:T(1,128)} %bitcast.5, s32[1,4,8]{2,1,0:T(4,128)} %bitcast.4, s32[8]{0:T(128)} %points_ref.1, f32[10]{0:T(128)} %emit_ref.1, f32[10]{0:T(128)} %settle_ref.1, f32[10]{0:T(128)} %mass_ref.1, ...), custom_call_target="tpu_custom_call" | custom-call | tf_op jit(solution)/shard_map/mix_and_exchange/pallas_call | solution.py:245
  48.2 8.9 %transform.1 = (f32[2,10,8,2,1280]{4,3,2,1,0:T(2,128)}, f32[8,256]{1,0:T(8,128)}) custom-call(bf16[16,2,10,8,256]{4,3,2,1,0:T(8,128)(2,1)} %get-tuple-element.4.x_ref, f32[16,2,256]{2,1,0:T(2,128)} %constant.4.clone.twiddle_ref, bf16[512,256]{1,0:T(8,128)(2,1)} %constant.9.table_ref, f32[8,256]{1,0:T(8,128)} %get-tuple-element.5.salt_in_ref), custom_call_target="tpu_custom_call" | custom-call | tf_op jit(solution)/shard_map/transform/pallas_call | solution.py:381

commit v2 on v1

--- a/solution.py
+++ b/solution.py
@@ -18,10 +18,26 @@
 ROWS = 8
 CHUNK = 2
 NCHUNK = NBD // CHUNK
+ORDER = (8, 4, 12, 6, 10, 7, 9, 5, 11, 3, 13, 2, 14, 1, 15)
 MESH = pl.DeviceIdType.MESH
 
 
-def mix_kernel(
+def fused_kernel(
+    ocean_hbm,
+    sea_hbm,
+    src_hbm,
+    points_hbm,
+    emit_hbm,
+    settle_hbm,
+    mass_hbm,
+    wind_hbm,
+    weights_hbm,
+    conc_hbm,
+    kdiff_hbm,
+    twiddle_hbm,
+    table_hbm,
+    spectra_hbm,
+    salt_ref,
     ocean_ref,
     sea_ref,
     src_ref,
@@ -29,24 +45,24 @@
     emit_ref,
     settle_ref,
     mass_ref,
-    wind_hbm,
-    weights_hbm,
-    conc_hbm,
-    kdiff_hbm,
-    recv_hbm,
-    salt_ref,
     wind_ref,
     weights_ref,
     conc_ref,
     kdiff_ref,
+    twiddle_ref,
+    table_ref,
     near_ref,
     lhs_ref,
     fields_ref,
     ratio_ref,
     scaled_ref,
     out_ref,
+    recv_ref,
     part_ref,
     other_ref,
+    z_ref,
+    o_ref,
+    y_ref,
     local_sem,
     own_sem,
     near_send,
@@ -55,6 +71,7 @@
     salt_recv,
     a2a_send,
     a2a_recv,
+    y_sem,
 ):
     sec = lax.axis_index("sec")
     lat = lax.axis_index("lat")
@@ -68,15 +85,32 @@
         peer = lax.rem(lon + shift + TILES, TILES)
         pl.semaphore_signal(barrier, inc=1, device_id=(1 - sec, lat, peer), device_id_type=MESH)
 
-    loads = [
-        pltpu.make_async_copy(kdiff_hbm, kdiff_ref, local_sem.at[0]),
-        pltpu.make_async_copy(conc_hbm, conc_ref, local_sem.at[1]),
-        pltpu.make_async_copy(weights_hbm, weights_ref, local_sem.at[2]),
-        pltpu.make_async_copy(wind_hbm, wind_ref, local_sem.at[3]),
+    ocean_load, sea_load, src_load, points_load, *rest = [
+        pltpu.make_async_copy(source, target, local_sem.at[i])
+        for i, (source, target) in enumerate(
+            [
+                (ocean_hbm, ocean_ref),
+                (sea_hbm, sea_ref),
+                (src_hbm, src_ref),
+                (points_hbm, points_ref),
+                (emit_hbm, emit_ref),
+                (settle_hbm, settle_ref),
+                (mass_hbm, mass_ref),
+                (kdiff_hbm, kdiff_ref),
+                (conc_hbm, conc_ref),
+                (wind_hbm, wind_ref),
+                (weights_hbm, weights_ref),
+                (twiddle_hbm, twiddle_ref),
+                (table_hbm, table_ref),
+            ]
+        )
     ]
-    for load in loads:
+    emit_load, settle_load, mass_load, kdiff_load, conc_load, wind_load, weights_load, *tables = rest
+    for load in (ocean_load, sea_load, src_load, points_load, *rest):
         load.start()
 
+    ocean_load.wait()
+    sea_load.wait()
     own_slot = sec * 6 + 2
     ocean = ocean_ref[...].astype(jnp.float32)
     for block in range(2):
@@ -106,8 +140,8 @@
             near_copies.append(copy)
             index += 1
 
-    loads[0].wait()
-    loads[1].wait()
+    kdiff_load.wait()
+    conc_load.wait()
 
     def eliminate(level, carried):
         ratio_prev, scaled_prev = carried
@@ -128,13 +162,14 @@
 
     row_ids = lax.broadcasted_iota(jnp.int32, (ROWS, PTS), 0)
     columns = lax.broadcasted_iota(jnp.int32, (ROWS, PTS), 1) + lon * PTS
+    points_load.wait()
     limits = jnp.zeros((ROWS, PTS), jnp.int32)
     for r in range(ROWS):
         limits = jnp.where(row_ids == r, points_ref[r], limits)
     valid = (columns < limits).astype(jnp.float32)
 
-    loads[2].wait()
-    loads[3].wait()
+    for load in (src_load, emit_load, settle_load, mass_load, wind_load, weights_load):
+        load.wait()
     for copy in near_copies:
         copy.wait()
 
@@ -186,7 +221,7 @@
         bins = pl.ds(chunk * CHUNK, CHUNK)
         return pltpu.make_async_remote_copy(
             src_ref=out_ref.at[pl.ds(peer * 2, 2), bins],
-            dst_ref=recv_hbm.at[lon, :, bins],
+            dst_ref=recv_ref.at[lon, :, bins],
             send_sem=a2a_send.at[chunk, step],
             recv_sem=a2a_recv.at[chunk, step],
             device_id=(sec, lat, peer),
@@ -196,17 +231,19 @@
     def own_copy(chunk):
         bins = pl.ds(chunk * CHUNK, CHUNK)
         return pltpu.make_async_copy(
-            out_ref.at[pl.ds(lon * 2, 2), bins], recv_hbm.at[lon, :, bins], own_sem.at[chunk]
+            out_ref.at[pl.ds(lon * 2, 2), bins], recv_ref.at[lon, :, bins], own_sem.at[chunk]
         )
 
     keep = valid > 0.0
-    for chunk in range(NCHUNK):
+
+    @pl.loop(0, NCHUNK)
+    def _(chunk):
         first = chunk * CHUNK
         start = tuple(scaled_ref[LEV - 1, first + b] for b in range(CHUNK))
         for b in range(CHUNK):
             out_ref[LEV - 1, first + b] = jnp.where(keep, start[b], 0.0).astype(jnp.bfloat16)
 
-        def substitute(count, carried, first=first):
+        def substitute(count, carried):
             level = LEV - 2 - count
             ratio = ratio_ref[level]
             values = []
@@ -217,54 +254,90 @@
             return tuple(values)
 
         lax.fori_loop(0, LEV - 1, substitute, start)
-        if chunk == 0:
+
+        @pl.when(chunk == 0)
+        def _():
             salt_copy.start()
 
-        @pl.loop(1, TILES)
-        def _(step, chunk=chunk):
+        for step in ORDER:
             a2a_copy(chunk, step).start()
-
         own_copy(chunk).start()
 
+    for load in tables:
+        load.wait()
     salt_copy.wait()
     salt_ref[...] = (part_ref[...] + other_ref[...]) * valid
 
-    for chunk in range(NCHUNK):
+    def y_copy(chunk, part):
+        return pltpu.make_async_copy(
+            y_ref.at[part], spectra_hbm.at[part, pl.ds(chunk * CHUNK, CHUNK)], y_sem.at[part]
+        )
+
+    @pl.loop(0, NCHUNK)
+    def _(chunk):
         own_copy(chunk).wait()
-
-        @pl.loop(1, TILES)
-        def _(step, chunk=chunk):
+        for step in ORDER:
             a2a_copy(chunk, step).wait()
-
-
-def mix_and_exchange(ocean, sea, src, points, emit, settle, mass, wind, weights, conc, kdiff):
+        for part in range(2):
+
+            @pl.when(chunk > 0)
+            def _():
+                y_copy(chunk - 1, part).wait()
+
+            transform(
+                recv_ref.at[:, part, pl.ds(chunk * CHUNK, CHUNK)],
+                twiddle_ref,
+                table_ref,
+                y_ref.at[part],
+                z_ref,
+                o_ref,
+            )
+            y_copy(chunk, part).start()
+
+    for part in range(2):
+        y_copy(NCHUNK - 1, part).wait()
+
+
+def fused(*operands):
     vmem = pl.BlockSpec(memory_space=pltpu.VMEM)
-    smem = pl.BlockSpec(memory_space=pltpu.SMEM)
     anywhere = pl.BlockSpec(memory_space=pl.ANY)
     dma = pltpu.SemaphoreType.DMA
     return pl.pallas_call(
-        mix_kernel,
-        name="mix_and_exchange",
+        fused_kernel,
+        name="fused",
         out_shape=(
-            jax.ShapeDtypeStruct((TILES, 2, NBD, ROWS, PTS), jnp.bfloat16),
+            jax.ShapeDtypeStruct((2, NBD, ROWS, 2, K), jnp.float32),
             jax.ShapeDtypeStruct((ROWS, PTS), jnp.float32),
         ),
-        in_specs=[vmem] + [smem] * 6 + [anywhere] * 4,
+        in_specs=[anywhere] * 13,
         out_specs=(anywhere, vmem),
         scratch_shapes=[
+            pltpu.VMEM((4, 2, 128), jnp.bfloat16),
+            pltpu.SMEM((1, 2), jnp.int32),
+            pltpu.SMEM((1, 4, 8), jnp.int32),
+            pltpu.SMEM((ROWS,), jnp.int32),
+            pltpu.SMEM((NBD,), jnp.float32),
+            pltpu.SMEM((NBD,), jnp.float32),
+            pltpu.SMEM((NBD,), jnp.float32),
             pltpu.VMEM((2, ROWS, PTS), jnp.float32),
             pltpu.VMEM((ROWS, 4, 128, PTS), jnp.bfloat16),
             pltpu.VMEM((LEV, NBD, ROWS, PTS), jnp.bfloat16),
             pltpu.VMEM((LEV, ROWS, PTS), jnp.float32),
+            pltpu.VMEM((TILES, 2, PTS), jnp.float32),
+            pltpu.VMEM((4 * PTS, 256), jnp.bfloat16),
             pltpu.VMEM((12, 8, 128), jnp.float32),
             pltpu.VMEM((ROWS, 8, 512), jnp.float32),
             pltpu.VMEM((ROWS, 8, PTS), jnp.float32),
             pltpu.VMEM((LEV, ROWS, PTS), jnp.float32),
             pltpu.VMEM((LEV, NBD, ROWS, PTS), jnp.float32),
             pltpu.VMEM((LEV, NBD, ROWS, PTS), jnp.bfloat16),
+            pltpu.VMEM((TILES, 2, NBD, ROWS, PTS), jnp.bfloat16),
             pltpu.VMEM((ROWS, PTS), jnp.float32),
             pltpu.VMEM((ROWS, PTS), jnp.float32),
-            dma((4,)),
+            pltpu.VMEM((TILES, 16, 4 * PTS), jnp.bfloat16),
+            pltpu.VMEM((TILES, 16, 256), jnp.float32),
+            pltpu.VMEM((2, CHUNK, ROWS, 2, K), jnp.float32),
+            dma((13,)),
             dma((NCHUNK,)),
             dma((5,)),
             dma((5,)),
@@ -272,9 +345,10 @@
             dma,
             dma((NCHUNK, TILES)),
             dma((NCHUNK, TILES)),
+            dma((2,)),
         ],
         compiler_params=pltpu.CompilerParams(collective_id=0, has_side_effects=True),
-    )(ocean, sea, src, points, emit, settle, mass, wind, weights, conc, kdiff)
+    )(*operands)
 
 
 def twiddles():
@@ -323,12 +397,11 @@
     return out
 
 
-def transform_kernel(x_ref, twiddle_ref, table_ref, salt_in_ref, y_ref, salt_ref, z_ref, o_ref):
-    salt_ref[...] = salt_in_ref[...]
+def transform(x_ref, twiddle_ref, table_ref, y_ref, z_ref, o_ref):
     for half in range(2):
         lanes = slice(half * 128, (half + 1) * 128)
         x = [
-            x_ref[tile, 0, :, :, lanes].astype(jnp.float32).reshape(16, 128)
+            x_ref[tile, :, :, lanes].astype(jnp.float32).reshape(16, 128)
             for tile in range(TILES)
         ]
         coefficients = real_dft16(x)
@@ -342,10 +415,14 @@
                 real, minus = re * cos - im * sin, re * sin + im * cos
             else:
                 real, minus = re * cos + im * sin, re * sin - im * cos
-            z_ref[kb, :, half * 128 : (half + 1) * 128] = real.astype(jnp.bfloat16)
-            z_ref[kb, :, PTS + half * 128 : PTS + (half + 1) * 128] = minus.astype(jnp.bfloat16)
+            for part, value in enumerate((real, minus)):
+                high = value.astype(jnp.bfloat16)
+                low = (value - high.astype(jnp.float32)).astype(jnp.bfloat16)
+                at = part * PTS + half * 128
+                z_ref[kb, :, at : at + 128] = high
+                z_ref[kb, :, 2 * PTS + at : 2 * PTS + at + 128] = low
     o_ref[...] = jnp.dot(
-        z_ref[...].reshape(TILES * 16, 2 * PTS), table_ref[...], preferred_element_type=jnp.float32
+        z_ref[...].reshape(TILES * 16, 4 * PTS), table_ref[...], preferred_element_type=jnp.float32
     ).reshape(TILES, 16, 256)
     lane = lax.broadcasted_iota(jnp.int32, (8, 128), 1)
     for group in range(2):
@@ -373,34 +450,7 @@
                 if t:
                     value = pltpu.roll(value, 128 - t, axis=1)
                 c, part = divmod(q * 16 + t, 2)
-                y_ref[0, group, :, part, c * 128 : (c + 1) * 128] = value
-
-
-def transform(received, salt):
-    whole = lambda *shape: pl.BlockSpec(shape, lambda i, j: (0,) * len(shape))
-    return pl.pallas_call(
-        transform_kernel,
-        name="transform",
-        grid=(2, NBD // 2),
-        out_shape=(
-            jax.ShapeDtypeStruct((2, NBD, ROWS, 2, K), jnp.float32),
-            jax.ShapeDtypeStruct((ROWS, PTS), jnp.float32),
-        ),
-        in_specs=[
-            pl.BlockSpec((TILES, 1, 2, ROWS, PTS), lambda i, j: (0, i, j, 0, 0)),
-            whole(TILES, 2, PTS),
-            whole(2 * PTS, 256),
-            whole(ROWS, PTS),
-        ],
-        out_specs=(
-            pl.BlockSpec((1, 2, ROWS, 2, K), lambda i, j: (i, j, 0, 0, 0)),
-            whole(ROWS, PTS),
-        ),
-        scratch_shapes=[
-            pltpu.VMEM((TILES, 16, 2 * PTS), jnp.bfloat16),
-            pltpu.VMEM((TILES, 16, 256), jnp.float32),
-        ],
-    )(received, jnp.asarray(twiddles()), jnp.asarray(row_table()).astype(jnp.bfloat16), salt)
+                y_ref[group, :, part, c * 128 : (c + 1) * 128] = value
 
 
 def on_device(
@@ -416,7 +466,8 @@
     bin_settle,
     bin_mass,
 ):
-    received, salt = mix_and_exchange(
+    table = jnp.asarray(row_table()).astype(jnp.bfloat16)
+    return fused(
         ocean_state.reshape(4, 2, 128),
         sea_tiles.reshape(1, 2),
         jnp.transpose(regrid_src, (1, 2, 0)),
@@ -428,8 +479,9 @@
         regrid_weights,
         conc,
         kdiff,
+        jnp.asarray(twiddles()),
+        jnp.concatenate([table, table], axis=0),
     )
-    return transform(received, salt)
 
 
 def solution(mesh):

time: 57.4 us -> 54.2 us (0.944)
  Pallas kernels: 56.5 us -> 49.4 us
  local copies, waits for them, and re-layouts: 0 us -> 3.78 us
    pallas_call x2 -> x1, Pallas kernels: 56.5 us -> 49.4 us  [fused(): pl.pallas_call(fused_kernel, name='fused', out_shape=(jax.ShapeDtypeStruc...]
    unnamed x0 -> x4, local copies, waits for them, and re-layouts: none -> 3.78 us
where the time goes in v2:
time: 54.2 us; the launch traced here: 53.9 us
  Pallas kernels  49.4 us (91%)
  local copies, waits for them, and re-layouts  3.78 us (7%)
  between operations  0.65 us (1%)
    pallas_call x1, Pallas kernels, fused(): pl.pallas_call(fused_kernel, name='fused', out_shape=(jax.ShapeDtypeStruc...  49.4 us
    unnamed x4, local copies, waits for them, and re-layouts  3.78 us

profile of v2, /device:TPU:16, one launch (start us, length us, event | category | flops | bytes accessed | tf_op | source)
XLA Modules:
  0.0 53.9 jit_solution(10020981096875572656)
XLA Ops:
  0.6 49.4 %fused.1 = (f32[2,10,8,2,1280]{4,3,2,1,0:T(2,128)}, f32[8,256]{1,0:T(8,128)}) custom-call(bf16[4,2,128]{2,1,0:T(2,128)(2,1)} %bitcast.3, s32[1,2]{1,0:T(1,128)} %bitcast.5, s32[1,4,8]{2,1,0:T(4,128)} %bitcast.4, s32[8]{0:T(128)} %points_hbm.1, f32[10]{0:T(128)} %emit_hbm.1, f32[10]{0:T(128)} %settle_hbm.1, f32[10]{0:T(128)} %mass_hbm.1, ...), custom_call_target="tpu_custom_call" | custom-call | tf_op jit(solution)/shard_map/fused/pallas_call | solution.py:305
  50.1 0.0 copy-start
  50.1 3.2 %copy.17 = f32[2,10,8,2,1280]{4,3,2,1,0:T(2,128)} copy(f32[2,10,8,2,1280]{4,3,2,1,0:T(2,128)} %get-tuple-element.4) | data formatting | bytes 3276800
  53.3 0.0 copy-done
  53.3 0.6 %copy.18 = f32[8,256]{1,0:T(8,128)} copy(f32[8,256]{1,0:T(8,128)S(1)} %copy-done) | data formatting | bytes 16384
Async XLA Ops:
  50.1 3.2 %copy-start = (f32[8,256]{1,0:T(8,128)S(1)}, f32[8,256]{1,0:T(8,128)}, u32[]{:S(2)}) copy-start(f32[8,256]{1,0:T(8,128)} %get-tuple-element.5) | copy-start | bytes 24580

commit v3 on v2

--- a/solution.py
+++ b/solution.py
@@ -16,10 +16,18 @@
 PTS = 256
 NBD = 10
 ROWS = 8
-CHUNK = 2
-NCHUNK = NBD // CHUNK
-ORDER = (8, 4, 12, 6, 10, 7, 9, 5, 11, 3, 13, 2, 14, 1, 15)
+ORDER = (10, 9, 11, 8, 6, 14, 5, 13, 7, 15, 4, 12, 2, 1, 3)
 MESH = pl.DeviceIdType.MESH
+
+
+def peer_of(lon, step):
+    z = lax.rem(lon // 4 + step // 4, 4)
+    x = lax.rem(lon % 4 + step % 4, 4)
+    return z * 4 + x
+
+
+def far(step):
+    return step // 4 == 2 and step % 4 != 0
 
 
 def fused_kernel(
@@ -36,7 +44,7 @@
     kdiff_hbm,
     twiddle_hbm,
     table_hbm,
-    spectra_hbm,
+    spectra_ref,
     salt_ref,
     ocean_ref,
     sea_ref,
@@ -62,7 +70,6 @@
     other_ref,
     z_ref,
     o_ref,
-    y_ref,
     local_sem,
     own_sem,
     near_send,
@@ -71,16 +78,20 @@
     salt_recv,
     a2a_send,
     a2a_recv,
-    y_sem,
+    row_sem,
 ):
     sec = lax.axis_index("sec")
     lat = lax.axis_index("lat")
     lon = lax.axis_index("lon")
 
     barrier = pltpu.get_barrier_semaphore()
+    greeted = 3
     for step in range(1, TILES):
-        peer = lax.rem(lon + step, TILES)
+        if far(step):
+            continue
+        peer = peer_of(lon, step)
         pl.semaphore_signal(barrier, inc=1, device_id=(sec, lat, peer), device_id_type=MESH)
+        greeted += 1
     for shift in (-1, 0, 1):
         peer = lax.rem(lon + shift + TILES, TILES)
         pl.semaphore_signal(barrier, inc=1, device_id=(1 - sec, lat, peer), device_id_type=MESH)
@@ -118,7 +129,10 @@
         sea = sea_ref[0, block].astype(jnp.float32)
         near_ref[own_slot + block, 0:4, :] = ocean[:, block, :] * sea
 
-    pl.semaphore_wait(barrier, TILES - 1 + 3)
+    pl.semaphore_wait(barrier, greeted)
+    pl.semaphore_signal(
+        row_sem, inc=1, device_id=(sec, lat, peer_of(lon, 8)), device_id_type=MESH
+    )
 
     near_copies = []
     index = 0
@@ -216,86 +230,86 @@
         device_id_type=MESH,
     )
 
-    def a2a_copy(chunk, step):
-        peer = lax.rem(lon + step, TILES)
-        bins = pl.ds(chunk * CHUNK, CHUNK)
+    def a2a_copy(b, step):
+        peer = peer_of(lon, step)
         return pltpu.make_async_remote_copy(
-            src_ref=out_ref.at[pl.ds(peer * 2, 2), bins],
-            dst_ref=recv_ref.at[lon, :, bins],
-            send_sem=a2a_send.at[chunk, step],
-            recv_sem=a2a_recv.at[chunk, step],
+            src_ref=out_ref.at[pl.ds(peer * 2, 2), b],
+            dst_ref=recv_ref.at[lon, :, b],
+            send_sem=a2a_send.at[b, step],
+            recv_sem=a2a_recv.at[b, step],
             device_id=(sec, lat, peer),
             device_id_type=MESH,
         )
 
-    def own_copy(chunk):
-        bins = pl.ds(chunk * CHUNK, CHUNK)
+    def own_copy(b):
         return pltpu.make_async_copy(
-            out_ref.at[pl.ds(lon * 2, 2), bins], recv_ref.at[lon, :, bins], own_sem.at[chunk]
+            out_ref.at[pl.ds(lon * 2, 2), b], recv_ref.at[lon, :, b], own_sem.at[b]
         )
 
     keep = valid > 0.0
-
-    @pl.loop(0, NCHUNK)
-    def _(chunk):
-        first = chunk * CHUNK
-        start = tuple(scaled_ref[LEV - 1, first + b] for b in range(CHUNK))
-        for b in range(CHUNK):
-            out_ref[LEV - 1, first + b] = jnp.where(keep, start[b], 0.0).astype(jnp.bfloat16)
-
-        def substitute(count, carried):
+    pl.semaphore_wait(row_sem, 1)
+
+    @pl.loop(0, NBD)
+    def _(b):
+        start = scaled_ref[LEV - 1, b]
+        out_ref[LEV - 1, b] = jnp.where(keep, start, 0.0).astype(jnp.bfloat16)
+
+        def substitute(count, below):
             level = LEV - 2 - count
-            ratio = ratio_ref[level]
-            values = []
-            for b in range(CHUNK):
-                value = scaled_ref[level, first + b] + ratio * carried[b]
-                out_ref[level, first + b] = jnp.where(keep, value, 0.0).astype(jnp.bfloat16)
-                values.append(value)
-            return tuple(values)
+            value = scaled_ref[level, b] + ratio_ref[level] * below
+            out_ref[level, b] = jnp.where(keep, value, 0.0).astype(jnp.bfloat16)
+            return value
 
         lax.fori_loop(0, LEV - 1, substitute, start)
 
-        @pl.when(chunk == 0)
+        @pl.when(b == 0)
         def _():
             salt_copy.start()
 
         for step in ORDER:
-            a2a_copy(chunk, step).start()
-        own_copy(chunk).start()
+            a2a_copy(b, step).start()
+        own_copy(b).start()
 
     for load in tables:
         load.wait()
     salt_copy.wait()
     salt_ref[...] = (part_ref[...] + other_ref[...]) * valid
 
-    def y_copy(chunk, part):
-        return pltpu.make_async_copy(
-            y_ref.at[part], spectra_hbm.at[part, pl.ds(chunk * CHUNK, CHUNK)], y_sem.at[part]
+    @pl.loop(0, NBD)
+    def _(b):
+        own_copy(b).wait()
+        for step in ORDER:
+            a2a_copy(b, step).wait()
+        transform(recv_ref.at[:, :, b], twiddle_ref, table_ref, spectra_ref.at[:, b], z_ref, o_ref)
+
+
+def deliver_kernel(from_spectra, from_salt, to_spectra, to_salt, sems):
+    copies = [
+        pltpu.make_async_copy(
+            from_spectra.at[part, pl.ds(5 * i, 5)], to_spectra.at[part, pl.ds(5 * i, 5)], sems.at[2 * part + i]
         )
-
-    @pl.loop(0, NCHUNK)
-    def _(chunk):
-        own_copy(chunk).wait()
-        for step in ORDER:
-            a2a_copy(chunk, step).wait()
-        for part in range(2):
-
-            @pl.when(chunk > 0)
-            def _():
-                y_copy(chunk - 1, part).wait()
-
-            transform(
-                recv_ref.at[:, part, pl.ds(chunk * CHUNK, CHUNK)],
-                twiddle_ref,
-                table_ref,
-                y_ref.at[part],
-                z_ref,
-                o_ref,
-            )
-            y_copy(chunk, part).start()
-
-    for part in range(2):
-        y_copy(NCHUNK - 1, part).wait()
+        for part in range(2)
+        for i in range(2)
+    ]
+    copies.append(pltpu.make_async_copy(from_salt, to_salt, sems.at[4]))
+    for copy in copies:
+        copy.start()
+    for copy in copies:
+        copy.wait()
+
+
+def deliver(spectra, salt):
+    anywhere = pl.BlockSpec(memory_space=pl.ANY)
+    vmem = pl.BlockSpec(memory_space=pltpu.VMEM)
+    return pl.pallas_call(
+        deliver_kernel,
+        name="deliver",
+        out_shape=tuple(jax.ShapeDtypeStruct(a.shape, a.dtype) for a in (spectra, salt)),
+        in_specs=[anywhere] * 2,
+        out_specs=(anywhere, anywhere),
+        scratch_shapes=[pltpu.SemaphoreType.DMA((5,))],
+        compiler_params=pltpu.CompilerParams(vmem_limit_bytes=2**20),
+    )(spectra, salt)
 
 
 def fused(*operands):
@@ -309,8 +323,8 @@
             jax.ShapeDtypeStruct((2, NBD, ROWS, 2, K), jnp.float32),
             jax.ShapeDtypeStruct((ROWS, PTS), jnp.float32),
         ),
-        in_specs=[anywhere] * 13,
-        out_specs=(anywhere, vmem),
+        in_specs=[pl.BlockSpec(memory_space=pltpu.HBM)] * 13,
+        out_specs=(vmem, vmem),
         scratch_shapes=[
             pltpu.VMEM((4, 2, 128), jnp.bfloat16),
             pltpu.SMEM((1, 2), jnp.int32),
@@ -336,19 +350,20 @@
             pltpu.VMEM((ROWS, PTS), jnp.float32),
             pltpu.VMEM((TILES, 16, 4 * PTS), jnp.bfloat16),
             pltpu.VMEM((TILES, 16, 256), jnp.float32),
-            pltpu.VMEM((2, CHUNK, ROWS, 2, K), jnp.float32),
             dma((13,)),
-            dma((NCHUNK,)),
+            dma((NBD,)),
             dma((5,)),
             dma((5,)),
             dma,
             dma,
-            dma((NCHUNK, TILES)),
-            dma((NCHUNK, TILES)),
-            dma((2,)),
+            dma((NBD, TILES)),
+            dma((NBD, TILES)),
+            pltpu.SemaphoreType.REGULAR,
         ],
-        compiler_params=pltpu.CompilerParams(collective_id=0, has_side_effects=True),
-    )(*operands)
+        compiler_params=pltpu.CompilerParams(
+            collective_id=0, has_side_effects=True, vmem_limit_bytes=16 * 2**20
+        ),
+    )(*[pltpu.with_memory_space_constraint(a, pltpu.HBM) for a in operands])
 
 
 def twiddles():
@@ -467,7 +482,7 @@
     bin_mass,
 ):
     table = jnp.asarray(row_table()).astype(jnp.bfloat16)
-    return fused(
+    spectra, salt = fused(
         ocean_state.reshape(4, 2, 128),
         sea_tiles.reshape(1, 2),
         jnp.transpose(regrid_src, (1, 2, 0)),
@@ -482,6 +497,7 @@
         jnp.asarray(twiddles()),
         jnp.concatenate([table, table], axis=0),
     )
+    return deliver(spectra, salt)
 
 
 def solution(mesh):

time: 54.2 us -> 51 us (0.941)
  local copies, waits for them, and re-layouts: 3.78 us -> 0 us
    unnamed x4 -> x0, local copies, waits for them, and re-layouts: 3.78 us -> none
    pallas_call x0 -> x1, Pallas kernels: none -> 1.21 us  [deliver(): pl.pallas_call(deliver_kernel, name='deliver', out_shape=tuple((jax.Shape...]
    pallas_call x1, Pallas kernels: 49.4 us -> 48.4 us  [fused(): pl.pallas_call(fused_kernel, name='fused', out_shape=(jax.ShapeDtypeStruc...]
where the time goes in v3:
time: 51 us; the launch traced here: 50.2 us
  Pallas kernels  49.6 us (97%)
  between operations  0.64 us (1%)
    pallas_call x1, Pallas kernels, fused(): pl.pallas_call(fused_kernel, name='fused', out_shape=(jax.ShapeDtypeStruc...  48.4 us
    pallas_call x1, Pallas kernels, deliver(): pl.pallas_call(deliver_kernel, name='deliver', out_shape=tuple((jax.Shape...  1.21 us

profile of v3, /device:TPU:16, one launch (start us, length us, event | category | flops | bytes accessed | tf_op | source)
XLA Modules:
  0.0 50.2 jit_solution(10634538727442818282)
XLA Ops:
  0.6 48.4 %fused.1 = (f32[2,10,8,2,1280]{4,3,2,1,0:T(2,128)S(1)}, f32[8,256]{1,0:T(8,128)S(1)}) custom-call(bf16[4,2,128]{2,1,0:T(2,128)(2,1)} %bitcast.3, s32[1,2]{1,0:T(1,128)} %bitcast.5, s32[1,4,8]{2,1,0:T(4,128)} %bitcast.4, s32[8]{0:T(128)} %points_hbm.1, f32[10]{0:T(128)} %emit_hbm.1, f32[10]{0:T(128)} %settle_hbm.1, f32[10]{0:T(128)} %mass_hbm.1, ...), custom_call_target="tpu_custom_call" | custom-call | tf_op jit(solution)/shard_map/fused/pallas_call | solution.py:319
  49.0 1.2 %deliver.1 = (f32[2,10,8,2,1280]{4,3,2,1,0:T(2,128)}, f32[8,256]{1,0:T(8,128)}) custom-call(f32[2,10,8,2,1280]{4,3,2,1,0:T(2,128)S(1)} %get-tuple-element.4.from_spectra, f32[8,256]{1,0:T(8,128)S(1)} %get-tuple-element.5.from_salt), custom_call_target="tpu_custom_call" | custom-call | tf_op jit(solution)/shard_map/deliver/pallas_call | solution.py:304

commit v4 on v3

--- a/solution.py
+++ b/solution.py
@@ -71,7 +71,6 @@
     z_ref,
     o_ref,
     local_sem,
-    own_sem,
     near_send,
     near_recv,
     salt_send,
@@ -134,8 +133,6 @@
         row_sem, inc=1, device_id=(sec, lat, peer_of(lon, 8)), device_id_type=MESH
     )
 
-    near_copies = []
-    index = 0
     for same_sec in (True, False):
         for shift in (-1, 0, 1):
             if same_sec and shift == 0:
@@ -145,14 +142,12 @@
             copy = pltpu.make_async_remote_copy(
                 src_ref=near_ref.at[pl.ds(own_slot, 2)],
                 dst_ref=near_ref.at[pl.ds(sec * 6 + (1 - shift) * 2, 2)],
-                send_sem=near_send.at[index],
-                recv_sem=near_recv.at[index],
+                send_sem=near_send,
+                recv_sem=near_recv,
                 device_id=(to_sec, lat, peer),
                 device_id_type=MESH,
             )
             copy.start()
-            near_copies.append(copy)
-            index += 1
 
     kdiff_load.wait()
     conc_load.wait()
@@ -184,8 +179,9 @@
 
     for load in (src_load, emit_load, settle_load, mass_load, wind_load, weights_load):
         load.wait()
-    for copy in near_copies:
-        copy.wait()
+    five = near_ref.at[pl.ds(0, 10)]
+    pltpu.make_async_copy(five, five, near_recv).wait()
+    pltpu.make_async_copy(five, five, near_send).wait()
 
     for r in range(ROWS):
         for s in range(4):
@@ -235,15 +231,15 @@
         return pltpu.make_async_remote_copy(
             src_ref=out_ref.at[pl.ds(peer * 2, 2), b],
             dst_ref=recv_ref.at[lon, :, b],
-            send_sem=a2a_send.at[b, step],
-            recv_sem=a2a_recv.at[b, step],
+            send_sem=a2a_send,
+            recv_sem=a2a_recv.at[b],
             device_id=(sec, lat, peer),
             device_id_type=MESH,
         )
 
     def own_copy(b):
         return pltpu.make_async_copy(
-            out_ref.at[pl.ds(lon * 2, 2), b], recv_ref.at[lon, :, b], own_sem.at[b]
+            out_ref.at[pl.ds(lon * 2, 2), b], recv_ref.at[lon, :, b], a2a_recv.at[b]
         )
 
     keep = valid > 0.0
@@ -277,21 +273,19 @@
 
     @pl.loop(0, NBD)
     def _(b):
-        own_copy(b).wait()
-        for step in ORDER:
-            a2a_copy(b, step).wait()
+        arrived = recv_ref.at[:, :, b]
+        pltpu.make_async_copy(arrived, arrived, a2a_recv.at[b]).wait()
         transform(recv_ref.at[:, :, b], twiddle_ref, table_ref, spectra_ref.at[:, b], z_ref, o_ref)
+
+    sent = out_ref.at[pl.ds(0, 2 * (TILES - 1))]
+    pltpu.make_async_copy(sent, sent, a2a_send).wait()
 
 
 def deliver_kernel(from_spectra, from_salt, to_spectra, to_salt, sems):
     copies = [
-        pltpu.make_async_copy(
-            from_spectra.at[part, pl.ds(5 * i, 5)], to_spectra.at[part, pl.ds(5 * i, 5)], sems.at[2 * part + i]
-        )
-        for part in range(2)
-        for i in range(2)
+        pltpu.make_async_copy(from_spectra, to_spectra, sems.at[0]),
+        pltpu.make_async_copy(from_salt, to_salt, sems.at[1]),
     ]
-    copies.append(pltpu.make_async_copy(from_salt, to_salt, sems.at[4]))
     for copy in copies:
         copy.start()
     for copy in copies:
@@ -307,7 +301,7 @@
         out_shape=tuple(jax.ShapeDtypeStruct(a.shape, a.dtype) for a in (spectra, salt)),
         in_specs=[anywhere] * 2,
         out_specs=(anywhere, anywhere),
-        scratch_shapes=[pltpu.SemaphoreType.DMA((5,))],
+        scratch_shapes=[pltpu.SemaphoreType.DMA((2,))],
         compiler_params=pltpu.CompilerParams(vmem_limit_bytes=2**20),
     )(spectra, salt)
 
@@ -351,13 +345,12 @@
             pltpu.VMEM((TILES, 16, 4 * PTS), jnp.bfloat16),
             pltpu.VMEM((TILES, 16, 256), jnp.float32),
             dma((13,)),
-            dma((NBD,)),
-            dma((5,)),
-            dma((5,)),
             dma,
             dma,
-            dma((NBD, TILES)),
-            dma((NBD, TILES)),
+            dma,
+            dma,
+            dma,
+            dma((NBD,)),
             pltpu.SemaphoreType.REGULAR,
         ],
         compiler_params=pltpu.CompilerParams(

time: 51 us -> 48 us (0.941)
  Pallas kernels: 49.6 us -> 46.6 us
    pallas_call x1, Pallas kernels: 48.4 us -> 45.4 us  [fused(): pl.pallas_call(fused_kernel, name='fused', out_shape=(jax.ShapeDtypeStruc...]
where the time goes in v4:
time: 48 us; the launch traced here: 47.3 us
  Pallas kernels  46.6 us (97%)
  between operations  0.64 us (1%)
    pallas_call x1, Pallas kernels, fused(): pl.pallas_call(fused_kernel, name='fused', out_shape=(jax.ShapeDtypeStruc...  45.4 us
    pallas_call x1, Pallas kernels, deliver(): pl.pallas_call(deliver_kernel, name='deliver', out_shape=tuple((jax.Shape...  1.19 us

profile of v4, /device:TPU:16, one launch (start us, length us, event | category | flops | bytes accessed | tf_op | source)
XLA Modules:
  0.0 47.3 jit_solution(13435231461389668991)
XLA Ops:
  0.6 45.4 %fused.1 = (f32[2,10,8,2,1280]{4,3,2,1,0:T(2,128)S(1)}, f32[8,256]{1,0:T(8,128)S(1)}) custom-call(bf16[4,2,128]{2,1,0:T(2,128)(2,1)} %bitcast.3, s32[1,2]{1,0:T(1,128)} %bitcast.5, s32[1,4,8]{2,1,0:T(4,128)} %bitcast.4, s32[8]{0:T(128)} %points_hbm.1, f32[10]{0:T(128)} %emit_hbm.1, f32[10]{0:T(128)} %settle_hbm.1, f32[10]{0:T(128)} %mass_hbm.1, ...), custom_call_target="tpu_custom_call" | custom-call | tf_op jit(solution)/shard_map/fused/pallas_call | solution.py:313
  46.1 1.2 %deliver.1 = (f32[2,10,8,2,1280]{4,3,2,1,0:T(2,128)}, f32[8,256]{1,0:T(8,128)}) custom-call(f32[2,10,8,2,1280]{4,3,2,1,0:T(2,128)S(1)} %get-tuple-element.4.from_spectra, f32[8,256]{1,0:T(8,128)S(1)} %get-tuple-element.5.from_salt), custom_call_target="tpu_custom_call" | custom-call | tf_op jit(solution)/shard_map/deliver/pallas_call | solution.py:298
